TPU v7x, 128 devices: a whole 4x4x4 slice. The times are simulated.
128 devices in a mesh: span: 8 (over z, y_hi), slab: 16 (over y_lo, x, core).
Axes of the slice: x: 4, y: 4 (y_hi: 2, y_lo: 2; y = y_hi * 2 + y_lo), z: 4, core: 2. Of those that a mesh axis runs over, the one named last changes fastest.
Arguments:
- activations: bfloat16 [32, 128, 128, 128], P('span', 'slab'), may hold values from -24 to 24
- cotangent: bfloat16 [32, 128, 128, 128], P('span', 'slab'), may hold values from -6 to 6
- conv_weight: bfloat16 [3, 3, 3, 128, 128], replicated, may hold values from -0.109375 to 0.109375
- norm_gain: float32 [128], replicated, may hold values from 0.25 to 1.75
- norm_shift: float32 [128], replicated, may hold values from -3 to 3
Outputs:
- input_grad: bfloat16 [32, 128, 128, 128], P('span', 'slab')
- weight_grad: float32 [3, 3, 3, 128, 128], replicated
- gain_grad: float32 [128], replicated
- shift_grad: float32 [128], replicated
- bias_grad: float32 [128], replicated
All inputs are finite; a program needn't handle non-finite values.
Results may differ from a plain program's by a relative error of at most 0.0029.
Values may be sent and summed in bfloat16 or wider, within the bound.
A program may use at most 128 MiB of HBM per device.

v0:
```python
import functools

import jax
import jax.numpy as jnp
from jax import lax
from jax.sharding import Mesh
from jax.sharding import PartitionSpec as P

G = 32
SPAN = ("span_0", "span_1")
SLAB = ("slab_0", "slab_1", "slab_2")
SPAN_SLAB = ("span_0", "span_1", "slab_0", "slab_1", "slab_2")


def by_axis(x, axes):
    return functools.reduce(lax.psum, axes, x)


def passed_along(value, axis, steps):
    count = lax.axis_size(axis)
    first, last = (max(0, -steps), min(count, count - steps))
    return lax.ppermute(value, axis, [(source, source + steps) for source in range(first, last)])


def padded_2(x, sides, width):
    for axis, dim in sides:
        devices, length = (lax.axis_size(axis), x.shape[dim])
        up = [(i, (i + 1) % devices) for i in range(devices - 1)]
        down = [(j, i) for i, j in up]
        last = lax.slice_in_dim(x, length - width, length, axis=dim)
        first = lax.slice_in_dim(x, 0, width, axis=dim)
        before = lax.ppermute(last, axis, up)
        after = lax.ppermute(first, axis, down)
        x = jnp.concatenate([before, x, after], axis=dim)
    return x


def cut_along(x, dim, devices):
    lengths = x.shape
    tiles = x.reshape(*lengths[:dim], devices, lengths[dim] // devices, *lengths[dim + 1 :])
    return jnp.moveaxis(tiles, dim, 0)


def sent_and_summed(x, axis, dim):
    tiles = cut_along(x, dim, lax.axis_size(axis))
    arrived = lax.all_to_all(tiles, axis, split_axis=0, concat_axis=0, tiled=True)
    return arrived.sum(axis=0)


def sent_to_all(x, axis):
    copies = jnp.broadcast_to(x, (lax.axis_size(axis), *x.shape))
    return lax.all_to_all(copies, axis, split_axis=0, concat_axis=0, tiled=True)


def taken_together(x, axis):
    return sent_to_all(x, axis).sum(axis=0)


def laid_out(tiles, dim):
    lengths = list(tiles.shape[1:])
    lengths[dim] *= tiles.shape[0]
    return jnp.moveaxis(tiles, 0, dim).reshape(lengths)


def gathered_copies(x, axis, dim):
    return laid_out(sent_to_all(x, axis), dim)


def tap_columns(padded, time_start, row_start, time_count, row_count, col_count, col_starts):
    window = padded[time_start : time_start + time_count, row_start : row_start + row_count]
    pieces = [window[:, :, begin : begin + col_count] for begin in col_starts]
    return jnp.concatenate(pieces, axis=-1).reshape(time_count * row_count * col_count, -1)


def body(activations, cotangent, conv_weight, norm_gain, norm_shift):
    frame_count, row_count, col_count, channels = activations.shape
    group_size = channels // G
    cells = frame_count * lax.axis_size(SPAN) * row_count * lax.axis_size(SLAB) * col_count
    members = cells * group_size
    inputs = activations.astype(jnp.float32)
    first_sums, square_sums = (
        by_axis(jnp.sum(inputs, axis=(0, 1, 2)), SPAN_SLAB),
        by_axis(jnp.sum(inputs * inputs, axis=(0, 1, 2)), SPAN_SLAB),
    )
    group_mean = first_sums.reshape(G, group_size).sum(axis=1) / members
    variance = square_sums.reshape(G, group_size).sum(axis=1) / members - group_mean * group_mean
    inv_std = lax.rsqrt(variance + 1e-06)
    inv_chan = jnp.repeat(inv_std, group_size)
    normed = (inputs - jnp.repeat(group_mean, group_size)) * inv_chan
    scaled = normed * norm_gain + norm_shift
    activated = (scaled * jax.nn.sigmoid(scaled)).astype(jnp.bfloat16)
    cached = passed_along(activated[frame_count - 2 :], SPAN, 1)
    act_time = jnp.concatenate([cached, activated], axis=0)
    act_rim = padded_2(act_time, ((SLAB, 1),), 1)
    act_pad = jnp.pad(act_rim, ((0, 0), (0, 0), (1, 1), (0, 0)))
    grad_flat = cotangent.reshape(-1, channels)
    weight_rows = []
    for tap_time in range(3):
        for tap_row in range(3):
            columns = tap_columns(
                act_pad, tap_time, tap_row, frame_count, row_count, col_count, (0, 1, 2)
            )
            weight_rows.append(
                lax.dot_general(
                    columns, grad_flat, (((0,), (0,)), ((), ())), preferred_element_type=jnp.float32
                )
            )
    weight_local = jnp.concatenate(weight_rows, axis=0)
    share = sent_and_summed(weight_local, SLAB, 0)
    share = taken_together(share, SPAN)
    weight_whole = gathered_copies(share, SLAB, 0)
    ahead = passed_along(cotangent[:2], SPAN, -1)
    grad_time = jnp.concatenate([cotangent, ahead], axis=0)
    pad_before, pad_after, out_frames = (0, 0, frame_count)
    grad_rim = padded_2(grad_time, ((SLAB, 1),), 1)
    grad_pad = jnp.pad(grad_rim, ((pad_before, pad_after), (0, 0), (1, 1), (0, 0)))
    act_grad = jnp.zeros((out_frames * row_count * col_count, channels), jnp.float32)
    for tap_time in range(3):
        for tap_row in range(3):
            grad_cols = tap_columns(
                grad_pad, 2 - tap_time, 2 - tap_row, out_frames, row_count, col_count, (2, 1, 0)
            )
            stacked = jnp.concatenate(
                [conv_weight[tap_time, tap_row, tap_col].T for tap_col in range(3)], axis=0
            )
            act_grad = act_grad + jnp.dot(grad_cols, stacked, preferred_element_type=jnp.float32)
    act_grad = act_grad.reshape(out_frames, row_count, col_count, channels)
    sigma = jax.nn.sigmoid(scaled)
    pre_grad = act_grad * sigma * (1.0 + scaled * (1.0 - sigma))
    gain_sum, shift_sum, bias_sum = (
        by_axis(jnp.sum(pre_grad * normed, axis=(0, 1, 2)), SPAN_SLAB),
        by_axis(jnp.sum(pre_grad, axis=(0, 1, 2)), SPAN_SLAB),
        by_axis(jnp.sum(cotangent.astype(jnp.float32), axis=(0, 1, 2)), SPAN_SLAB),
    )
    mean_one = jnp.repeat(
        (norm_gain * shift_sum).reshape(G, group_size).sum(axis=1) / members, group_size
    )
    mean_two = jnp.repeat(
        (norm_gain * gain_sum).reshape(G, group_size).sum(axis=1) / members, group_size
    )
    input_grad = (inv_chan * (norm_gain * pre_grad - mean_one - normed * mean_two)).astype(
        jnp.bfloat16
    )
    factor = 1.0 / jnp.sqrt(jnp.float32(cells))
    weight_grad = weight_whole.reshape(3, 3, 3, channels, channels) * factor
    return (input_grad, weight_grad, gain_sum * factor, shift_sum * factor, bias_sum * factor)


def solution(mesh):
    split = Mesh(
        mesh.devices.reshape(4, 2, 2, 4, 2), ("span_0", "span_1", "slab_0", "slab_1", "slab_2")
    )
    placed = (P(SPAN, SLAB, None, None), P(SPAN, SLAB, None, None), P(), P(), P())
    return jax.shard_map(
        body,
        mesh=split,
        in_specs=placed,
        out_specs=(P(SPAN, SLAB, None, None), P(), P(), P(), P()),
        check_vma=False,
    )
```

profile of v0, /device:TPU:1, one launch (start us, length us, event | category | flops | bytes accessed | tf_op | source)
XLA Modules:
  0.0 250.4 jit_solution(3703023131212992762)
XLA Ops:
  0.7 2.0 slice.365
  2.7 1.3 collective-permute-start
  4.0 1.6 copy.16
  6.0 14.5 %all-reduce.5 = (f32[128]{0:T(128)S(1)}, f32[128]{0:T(128)S(1)}) all-reduce(f32[128]{0:T(128)S(1)} %get-tuple-element.23, f32[128]{0:T(128)S(1)} %get-tuple-element.22), channel_id=1, replica_groups=mesh['span_0'=4,'span_1'=2,'slab_0'=2,'slab_1'=4,'slab_2'=2] {'span_0'}, use_global_device_ids=true, to_apply=%region_8.0 | all-reduce | flops 256 | bytes 2048 | tf_op jit(solution)/shard_map/psum | solution.py:16
  20.5 5.3 %all-reduce.11 = (f32[128]{0:T(128)S(1)}, f32[128]{0:T(128)S(1)}) all-reduce(f32[128]{0:T(128)S(1)} %get-tuple-element.32, f32[128]{0:T(128)S(1)} %get-tuple-element.33), channel_id=1, replica_groups=mesh['span_0'=4,'span_1'=2,'slab_0'=2,'slab_1'=4,'slab_2'=2] {'span_1'}, use_global_device_ids=true, to_apply=%region_9.0 | all-reduce | flops 256 | bytes 2048 | tf_op jit(solution)/shard_map/psum | solution.py:16
  25.7 3.8 %all-reduce.9 = (f32[128]{0:T(128)S(1)}, f32[128]{0:T(128)S(1)}) all-reduce(f32[128]{0:T(128)S(1)} %get-tuple-element.47, f32[128]{0:T(128)S(1)} %get-tuple-element.48), channel_id=1, replica_groups=mesh['span_0'=4,'span_1'=2,'slab_0'=2,'slab_1'=4,'slab_2'=2] {'slab_0'}, use_global_device_ids=true, to_apply=%region_10.0 | all-reduce | flops 256 | bytes 2048 | tf_op jit(solution)/shard_map/psum | solution.py:16
  29.5 8.4 %all-reduce.3 = (f32[128]{0:T(128)S(1)}, f32[128]{0:T(128)S(1)}) all-reduce(f32[128]{0:T(128)S(1)} %get-tuple-element.42, f32[128]{0:T(128)S(1)} %get-tuple-element.43), channel_id=1, replica_groups=mesh['span_0'=4,'span_1'=2,'slab_0'=2,'slab_1'=4,'slab_2'=2] {'slab_1'}, use_global_device_ids=true, to_apply=%region_11.0 | all-reduce | flops 256 | bytes 2048 | tf_op jit(solution)/shard_map/psum | solution.py:16
  38.2 10.5 %all-reduce.7 = (f32[32,4]{1,0:T(8,128)S(1)}, f32[32,4]{1,0:T(8,128)}) all-reduce(f32[32,4]{1,0:T(8,128)S(1)} %reshape.74, f32[32,4]{1,0:T(8,128)S(1)} %reshape.73), channel_id=1, replica_groups=mesh['span_0'=4,'span_1'=2,'slab_0'=2,'slab_1'=4,'slab_2'=2] {'slab_2'}, use_global_device_ids=true, to_apply=%region_12.0 | all-reduce | flops 256 | bytes 2048 | tf_op jit(solution)/shard_map/psum | solution.py:16
  51.1 1.9 collective-permute-start.1
  53.0 2.4 collective-permute-start.2
  56.2 3.9 %collective-permute-done.2 = bf16[6,1,128,128]{3,2,1,0:T(8,128)(2,1)S(1)} collective-permute-done((bf16[6,1,128,128]{3,2,1,0:T(8,128)(2,1)S(1)}, bf16[6,1,128,128]{3,2,1,0:T(8,128)(2,1)S(1)}, u32[]{:S(2)}, u32[]{:S(2)}) %collective-permute-start.2) | collective-permute-done | bytes 196640 | tf_op jit(solution)/shard_map/ppermute | solution.py:33
  60.0 1.0 fusion.84
  61.1 5.7 %fusion.211 = (bf16[4,8,128,128]{3,2,1,0:T(8,128)(2,1)S(1)}, bf16[4,8,128,128]{3,2,1,0:T(8,128)(2,1)}, bf16[4,8,128,128]{3,2,1,0:T(8,128)(2,1)}, bf16[4,8,128,12...) fusion(bf16[6,10,130,128]{3,2,1,0:T(8,128)(2,1)S(1)} %fusion.84), kind=kLoop, calls=%fused_computation.252 | loop fusion | bytes 37748736 | tf_op jit(solution)/shard_map/slice | solution.py:71
  66.8 2.0 pad_maximum_fusion.9
  72.0 1.0 fusion.144
  73.0 1.0 convolution_add_fusion.7
  75.3 1.0 convolution_add_fusion.6
  76.4 1.1 convolution_add_fusion.5
  77.5 1.0 pad_maximum_fusion.7
  78.5 1.0 convolution_add_fusion.4
  79.6 1.0 convolution_add_fusion.3
  80.7 2.0 fusion.8
  82.8 1.0 convolution_add_fusion.2
  83.9 1.0 convolution_add_fusion.1
  84.9 1.1 convolution_add_fusion
  86.0 1.8 copy.17
  87.9 4.3 %fusion.208 = (f32[128]{0:T(128)S(1)}, f32[128]{0:T(128)S(1)}, f32[4,8,128,128]{2,3,1,0:T(8,128)}, bf16[4,8,128,128]{2,3,1,0:T(8,128)(2,1)S(1)}) fusion(f32[128]{0:T(128)S(1)} %mul.87, f32[128]{0:T(128)S(1)} %sub.30, bf16[4,8,128,128]{2,3,1,0:T(8,128)(2,1)S(1)} %copy.16, f32[4,8,128,128]{2,3,1,0:T(8,128)} %copy.17, f32[128]{0:T(128)S(1)} %copy-done.61, ...), kind=kLoop, calls=%fused_computation.250 | loop fusion | flops 9436928 | bytes 6294528 | tf_op jit(solution)/shard_map/reduce_sum | solution.py:132
  92.2 2.3 collective-permute-start.3
  94.6 9.0 %collective-permute-done.3 = bf16[2,8,128,128]{2,3,1,0:T(8,128)(2,1)S(1)} collective-permute-done((bf16[2,8,128,128]{2,3,1,0:T(8,128)(2,1)S(1)}, bf16[2,8,128,128]{2,3,1,0:T(8,128)(2,1)S(1)}, u32[]{:S(2)}, u32[]{:S(2)}) %collective-permute-start.3) | collective-permute-done | bytes 524320 | tf_op jit(solution)/shard_map/ppermute | solution.py:22
  103.6 5.2 %collective-permute-start.4 = (bf16[6,1,128,128]{2,3,1,0:T(8,128)(2,1)S(1)}, bf16[6,1,128,128]{2,3,1,0:T(8,128)(2,1)S(1)}, u32[]{:S(2)}, u32[]{:S(2)}) collective-permute-start(bf16[6,1,128,128]{2,3,1,0:T(8,128)(2,1)S(1)} %get-tuple-element.98), channel_id=1, source_target_pairs={{0,1},{1,2},{2,3},{3,4},{4,5},{5,6},{6,7},{7,8},{8,9},{9,10},{10,1... | collective-permute-start | bytes 589832 | tf_op jit(solution)/shard_map/ppermute | solution.py:32
  108.8 1.9 collective-permute-start.5
  110.7 1.1 fusion.139
  111.9 3.9 %collective-permute-done.5 = bf16[6,1,128,128]{2,3,1,0:T(8,128)(2,1)S(1)} collective-permute-done((bf16[6,1,128,128]{2,3,1,0:T(8,128)(2,1)S(1)}, bf16[6,1,128,128]{2,3,1,0:T(8,128)(2,1)S(1)}, u32[]{:S(2)}, u32[]{:S(2)}) %collective-permute-start.5) | collective-permute-done | bytes 196640 | tf_op jit(solution)/shard_map/ppermute | solution.py:33
  116.3 1.9 fusion.213
  118.2 3.0 %select_maximum_fusion = bf16[6,10,130,128]{2,3,1,0:T(8,128)(2,1)S(1)} fusion(bf16[6,1,128,128]{2,3,1,0:T(8,128)(2,1)S(1)} %collective-permute-done.5, bf16[6,1,128,128]{2,3,1,0:T(8,128)(2,1)S(1)} %collective-permute-done.4, bf16[4,8,128,128]{2,3,1,0:T(8,128)(2,1)S(1)} %get-tuple-element.108, bf16[2,8,128,128]{2,3,1,0:T(8,128)(2,1)S(1)} %collective-permute-done.3), kind=kLoop, calls=%fused_computation.14 | loop fusion | flops 14976000 | bytes 3962880 | tf_op jit(solution)/shard_map/concatenate | solution.py:34
  121.2 8.3 %fusion.210 = (bf16[4,8,128,128]{2,3,1,0:T(8,128)(2,1)}, bf16[4,8,128,128]{2,3,1,0:T(8,128)(2,1)}, bf16[4,8,128,128]{2,3,1,0:T(8,128)(2,1)}, bf16[4,8,128,128]{2...) fusion(bf16[6,10,130,128]{2,3,1,0:T(8,128)(2,1)S(1)} %select_ma, ...), kind=kLoop, calls=%fused_computation.251 | loop fusion | bytes 37748736 | tf_op jit(solution)/shard_map/slice | solution.py:71
  146.1 30.3 %all_to_all.15 = f32[16,216,128]{2,1,0:T(8,128)S(1)} all-to-all(f32[16,216,128]{2,1,0:T(8,128)S(1)} %bitcast.203), channel_id=1, replica_groups=mesh['span_0'=4,'span_1'=2,'slab_0'=2,'slab_1'=4,'slab_2'=2] {'slab_0','..., dimensions={0} | all-to-all | bytes 3538944 | tf_op jit(solution)/shard_map/all_to_all | solution.py:46
  176.6 20.4 %all_to_all.16 = f32[8,216,128]{2,1,0:T(8,128)S(1)} all-to-all(f32[8,216,128]{2,1,0:T(8,128)S(1)} %broadcast_in_dim.25), channel_id=1, replica_groups=mesh['span_0'=4,'span_1'=2,'slab_0'=2,'slab_1'=4,'slab_2'=2] {'span_0','..., dimensions={0} | all-to-all | bytes 1769472 | tf_op jit(solution)/shard_map/all_to_all | solution.py:52
  197.1 1.3 broadcast_in_dim.26
  198.4 5.9 %all-to-all-start.2 = ((f32[16,216,128]{2,1,0:T(8,128)}), f32[16,216,128]{2,1,0:T(8,128)}, u32[]{:S(2)}, u32[]{:S(2)}) async-start(f32[16,216,128]{2,1,0:T(8,128)} %broadcast_in_dim.26), calls=%async_computation.2 | async-start | bytes 3538944 | tf_op jit(solution)/shard_map/all_to_all | solution.py:52
  204.9 7.2 %all-reduce.4 = (f32[128]{0:T(128)S(1)}, f32[128]{0:T(128)S(1)}, f32[128]{0:T(128)S(1)}) all-reduce(f32[128]{0:T(128)S(1)} %get-tuple-element.21, f32[128]{0:T(128)S(1)} %get-tuple-element.20, f32[128]{0:T(128)S(1)} %convert_reduce_fusion.1), channel_id=1, replica_groups=mesh['span_0'=4,'span_1'=2,'slab_0'=2,'slab_1'=4,'slab_2'=2] {'span_0'}, use_global_device_ids=true, to_apply=%region_22.23 | all-reduce | flops 384 | bytes 3072 | tf_op jit(solution)/shard_map/psum | solution.py:16
  212.1 5.9 %all-reduce.10 = (f32[128]{0:T(128)S(1)}, f32[128]{0:T(128)S(1)}, f32[128]{0:T(128)S(1)}) all-reduce(f32[128]{0:T(128)S(1)} %get-tuple-element.29, f32[128]{0:T(128)S(1)} %get-tuple-element.30, f32[128]{0:T(128)S(1)} %get-tuple-element.31), channel_id=1, replica_groups=mesh['span_0'=4,'span_1'=2,'slab_0'=2,'slab_1'=4,'slab_2'=2] {'span_1'}, use_global_device_ids=true, to_apply=%region_23.24 | all-reduce | flops 384 | bytes 3072 | tf_op jit(solution)/shard_map/psum | solution.py:16
  218.0 6.7 %all-reduce.8 = (f32[128]{0:T(128)S(1)}, f32[128]{0:T(128)S(1)}, f32[128]{0:T(128)S(1)}) all-reduce(f32[128]{0:T(128)S(1)} %get-tuple-element.44, f32[128]{0:T(128)S(1)} %get-tuple-element.45, f32[128]{0:T(128)S(1)} %get-tuple-element.46), channel_id=1, replica_groups=mesh['span_0'=4,'span_1'=2,'slab_0'=2,'slab_1'=4,'slab_2'=2] {'slab_0'}, use_global_device_ids=true, to_apply=%region_24.25 | all-reduce | flops 384 | bytes 3072 | tf_op jit(solution)/shard_map/psum | solution.py:16
  224.7 11.1 %all-reduce.2 = (f32[128]{0:T(128)S(1)}, f32[128]{0:T(128)S(1)}, f32[128]{0:T(128)S(1)}) all-reduce(f32[128]{0:T(128)S(1)} %get-tuple-element.39, f32[128]{0:T(128)S(1)} %get-tuple-element.40, f32[128]{0:T(128)S(1)} %get-tuple-element.41), channel_id=1, replica_groups=mesh['span_0'=4,'span_1'=2,'slab_0'=2,'slab_1'=4,'slab_2'=2] {'slab_1'}, use_global_device_ids=true, to_apply=%region_25.26 | all-reduce | flops 384 | bytes 3072 | tf_op jit(solution)/shard_map/psum | solution.py:16
  235.8 6.3 %all-reduce.6 = (f32[128]{0:T(128)S(1)}, f32[128]{0:T(128)S(1)}, f32[128]{0:T(128)S(1)}) all-reduce(f32[128]{0:T(128)S(1)} %get-tuple-element.24, f32[128]{0:T(128)S(1)} %get-tuple-element.25, f32[128]{0:T(128)S(1)} %get-tuple-element.26), channel_id=1, replica_groups=mesh['span_0'=4,'span_1'=2,'slab_0'=2,'slab_1'=4,'slab_2'=2] {'slab_2'}, use_global_device_ids=true, to_apply=%region_26.27 | all-reduce | flops 384 | bytes 3072 | tf_op jit(solution)/shard_map/psum | solution.py:16
  243.4 2.3 fusion.82
  245.7 1.3 copy.18
  247.5 2.8 %broadcast_multiply_fusion = f32[16,216,128]{2,1,0:T(8,128)} fusion(f32[16,216,128]{2,1,0:T(8,128)} %all-to-all-done.2), kind=kLoop, calls=%fused_computation.147 | loop fusion | flops 442368 | bytes 3538944 | tf_op jit(solution)/shard_map/mul | solution.py:145
  (175 shorter events, 27.6 us)
Async XLA Ops:
  0.6 49.4 %copy-start = (bf16[4,8,128,128]{3,2,1,0:T(8,128)(2,1)S(1)}, bf16[4,8,128,128]{3,2,1,0:T(8,128)(2,1)}, u32[]{:S(2)}) copy-start(bf16[4,8,128,128]{3,2,1,0:T(8,128)(2,1)} %param.6) | copy-start | bytes 3145732
  0.6 49.5 %copy-start.32 = (bf16[3,3,3,128,128]{4,3,2,1,0:T(8,128)(2,1)S(1)}, bf16[3,3,3,128,128]{4,3,2,1,0:T(8,128)(2,1)}, u32[]{:S(2)}) copy-start(bf16[3,3,3,128,128]{4,3,2,1,0:T(8,128)(2,1)} %param.7) | copy-start | bytes 2654212
  2.7 48.3 %collective-permute-start = (bf16[2,8,128,128]{3,2,1,0:T(8,128)(2,1)}, bf16[2,8,128,128]{3,2,1,0:T(8,128)(2,1)S(1)}, u32[]{:S(2)}, u32[]{:S(2)}) collective-permute-start(bf16[2,8,128,128]{3,2,1,0:T(8,128)(2,1)} %slice.365), channel_id=1, source_target_pairs={{16,0},{32,16},{48,32},{64,48},{80,64},{96,80},{112,96},{17,1},{33... | collective-permute-start | bytes 1572872 | tf_op jit(solution)/shard_map/ppermute | solution.py:22
  51.1 5.1 %collective-permute-start.1 = (bf16[6,1,128,128]{3,2,1,0:T(8,128)(2,1)S(1)}, bf16[6,1,128,128]{3,2,1,0:T(8,128)(2,1)S(1)}, u32[]{:S(2)}, u32[]{:S(2)}) collective-permute-start(bf16[6,1,128,128]{3,2,1,0:T(8,128)(2,1)S(1)} %get-tuple-element.106), channel_id=1, source_target_pairs={{0,1},{1,2},{2,3},{3,4},{4,5},{5,6},{6,7},{7,8},{8,9},{9,10},{10,1... | collective-permute-start | bytes 589832 | tf_op jit(solution)/shard_map/ppermute | solution.py:32
  53.0 7.0 %collective-permute-start.2 = (bf16[6,1,128,128]{3,2,1,0:T(8,128)(2,1)S(1)}, bf16[6,1,128,128]{3,2,1,0:T(8,128)(2,1)S(1)}, u32[]{:S(2)}, u32[]{:S(2)}) collective-permute-start(bf16[6,1,128,128]{3,2,1,0:T(8,128)(2,1)S(1)} %get-tuple-element.107), channel_id=1, source_target_pairs={{1,0},{2,1},{3,2},{4,3},{5,4},{6,5},{7,6},{8,7},{9,8},{10,9},{11,1... | collective-permute-start | bytes 589832 | tf_op jit(solution)/shard_map/ppermute | solution.py:33
  68.8 1.2 copy-start.6
  68.8 1.5 copy-start.7
  68.8 1.8 copy-start.8
  68.9 2.1 copy-start.9
  73.0 1.2 copy-start.5
  75.3 1.1 copy-start.48
  75.3 1.1 copy-start.49
  75.3 1.1 copy-start.50
  78.5 1.1 copy-start.40
  80.7 2.1 copy-start.37
  80.7 2.1 copy-start.38
  80.7 2.1 copy-start.39
  86.0 1.9 copy-start.60
  86.0 1.9 copy-start.61
  92.2 11.4 %collective-permute-start.3 = (bf16[2,8,128,128]{2,3,1,0:T(8,128)(2,1)S(1)}, bf16[2,8,128,128]{2,3,1,0:T(8,128)(2,1)S(1)}, u32[]{:S(2)}, u32[]{:S(2)}) collective-permute-start(bf16[2,8,128,128]{2,3,1,0:T(8,128)(2,1)S(1)} %slice.480), channel_id=1, source_target_pairs={{0,16},{16,32},{32,48},{48,64},{64,80},{80,96},{96,112},{1,17},{17... | collective-permute-start | bytes 1572872 | tf_op jit(solution)/shard_map/ppermute | solution.py:22
  103.6 14.6 %copy-start.3 = (bf16[2,8,128,128]{2,3,1,0:T(8,128)(2,1)}, bf16[2,8,128,128]{2,3,1,0:T(8,128)(2,1)S(1)}, u32[]{:S(2)}) copy-start(bf16[2,8,128,128]{2,3,1,0:T(8,128)(2,1)S(1)} %collective-permute-done.3) | copy-start | bytes 1572868
  103.6 8.2 %collective-permute-start.4 = (bf16[6,1,128,128]{2,3,1,0:T(8,128)(2,1)S(1)}, bf16[6,1,128,128]{2,3,1,0:T(8,128)(2,1)S(1)}, u32[]{:S(2)}, u32[]{:S(2)}) collective-permute-start(bf16[6,1,128,128]{2,3,1,0:T(8,128)(2,1)S(1)} %get-tuple-element.98), channel_id=1, source_target_pairs={{0,1},{1,2},{2,3},{3,4},{4,5},{5,6},{6,7},{7,8},{8,9},{9,10},{10,1... | collective-permute-start | bytes 589832 | tf_op jit(solution)/shard_map/ppermute | solution.py:32
  108.8 7.0 %collective-permute-start.5 = (bf16[6,1,128,128]{2,3,1,0:T(8,128)(2,1)S(1)}, bf16[6,1,128,128]{2,3,1,0:T(8,128)(2,1)S(1)}, u32[]{:S(2)}, u32[]{:S(2)}) collective-permute-start(bf16[6,1,128,128]{2,3,1,0:T(8,128)(2,1)S(1)} %get-tuple-element.99), channel_id=1, source_target_pairs={{1,0},{2,1},{3,2},{4,3},{5,4},{6,5},{7,6},{8,7},{9,8},{10,9},{11,1... | collective-permute-start | bytes 589832 | tf_op jit(solution)/shard_map/ppermute | solution.py:33
  129.5 1.2 copy-start.1
  129.6 1.5 copy-start.26
  129.6 1.8 copy-start.27
  129.6 2.1 copy-start.31
  131.7 1.2 copy-start.24
  131.7 1.5 copy-start.25
  131.7 1.9 copy-start.28
  133.6 1.2 copy-start.22
  133.6 1.5 copy-start.23
  135.1 1.2 copy-start.20
  135.1 1.5 copy-start.21
  135.1 1.9 copy-start.30
  137.0 1.4 copy-start.18
  137.0 1.7 copy-start.19
  138.7 1.2 copy-start.16
  138.7 1.5 copy-start.17
  140.2 1.2 copy-start.14
  140.2 1.5 copy-start.15
  140.2 1.9 copy-start.29
  142.1 1.2 copy-start.12
  142.1 1.5 copy-start.13
  143.6 1.2 copy-start.10
  143.6 1.5 copy-start.11
  197.0 7.3 %copy-start.2 = (bf16[4,8,128,128]{3,2,1,0:T(8,128)(2,1)S(1)}, bf16[4,8,128,128]{3,2,1,0:T(8,128)(2,1)}, u32[]{:S(2)}) copy-start(bf16[4,8,128,128]{3,2,1,0:T(8,128)(2,1)} %param.6) | copy-start | bytes 3145732
  198.4 49.1 %all-to-all-start.2 = ((f32[16,216,128]{2,1,0:T(8,128)}), f32[16,216,128]{2,1,0:T(8,128)}, u32[]{:S(2)}, u32[]{:S(2)}) async-start(f32[16,216,128]{2,1,0:T(8,128)} %broadcast_in_dim.26), calls=%async_computation.2 | async-start | bytes 3538944 | tf_op jit(solution)/shard_map/all_to_all | solution.py:52
  (21 other events, 21.6 us)
where the time goes:
time: 251 us; the launch traced here: 250 us
  blocking collectives  130 us (52%)
  local copies, waits for them, and re-layouts  36.7 us (15%)
  other arithmetic  25.9 us (10%)
  starting transfers between devices  21 us (8%)
  matrix products  18 us (7%)
  waiting for transfers between devices  16.8 us (7%)
    psum x10, blocking collectives, by_axis(): return functools.reduce(lax.psum, axes, x)  79.7 us
    all_to_all x1, blocking collectives, sent_and_summed(): lax.all_to_all(tiles, axis, split_axis=0, concat_axis=0, tiled=True)  30.3 us
    all_to_all x1, blocking collectives, sent_to_all(): return lax.all_to_all(copies, axis, split_axis=0, concat_axis=0, tiled=True)  20.4 us
    slice x4, local copies, waits for them, and re-layouts, tap_columns(): pieces = [window[:, :, begin:begin + col_count] for begin in col_starts]  16.7 us
    unnamed x127, local copies, waits for them, and re-layouts  12 us
    dot_general x9, matrix products, body(): jnp.dot(grad_cols, stacked, preferred_element_type=jnp.float32)  9.27 us
    ppermute x2, waiting for transfers between devices, passed_along(): lax.ppermute(value, axis, [(source, source + steps) for source in range(f...  9.02 us
    dot_general x9, matrix products, body(): lax.dot_general(columns, grad_flat, (((0,), (0,)), ((), ())), preferred_e...  8.73 us
  transfers between devices with their start and end apart: 7, of which 3 were waited for; matrix products, arithmetic and copies ran while one was open for 5% of the time, Pallas kernels for 0%

commit v1 on v0

v1 whole, which is shorter than its diff:
```python
import functools

import jax
import jax.numpy as jnp
from jax import lax
from jax.experimental import pallas as pl
from jax.experimental.pallas import tpu as pltpu
from jax.sharding import PartitionSpec as P

MESH = pl.DeviceIdType.MESH
F32 = jnp.float32
BF16 = jnp.bfloat16
NF, NR, W, C = 4, 8, 128, 128
ROWS = NR * W
CELLS = 32 * 128 * 128
MEMBERS = CELLS * 4
SCALE = float(CELLS) ** -0.5
NT_DIMS = (((1,), (1,)), ((), ()))


def group_sum(v):
    lane = lax.broadcasted_iota(jnp.int32, v.shape, 1)
    v = v + jnp.where(lane % 2 == 0, pltpu.roll(v, C - 1, 1), pltpu.roll(v, 1, 1))
    return v + jnp.where(lane % 4 < 2, pltpu.roll(v, C - 2, 1), pltpu.roll(v, 2, 1))


def kernel(
    act_hbm, cot_hbm, w_hbm, gain_ref, shift_ref,
    out_hbm, wout_hbm, sums_ref,
    act_v, grad_v, w_v, at_v, ag_v, dv_v, wacc, rs_core, rs_axis, rs_own, rs_plane, wout, outb, stat, arb, ara,
    loc_sem, out_sem, halo_s, halo_r, arb_s, arb_r, ara_s, ara_r,
    c_s, c_r, x_s, x_r, p_s, p_r, gp_s, gp_r, gx_s, gx_r, gc_s, gc_r,
):
    span, slab = lax.axis_index("span"), lax.axis_index("slab")
    y_lo, xc = slab // 8, slab % 8
    x, core = xc // 2, xc % 2
    plane = span * 2 + y_lo

    def in_plane(q):
        return (q // 2, (q % 2) * 8 + xc)

    def in_row(j):
        return (span, y_lo * 8 + j)

    before, after = (span + 7) % 8, (span + 1) % 8
    above, below = (slab + 15) % 16, (slab + 1) % 16

    copy_act = pltpu.make_async_copy(act_hbm, act_v, loc_sem.at[0])
    copy_cot = pltpu.make_async_copy(cot_hbm, grad_v.at[pl.ds(0, NF), pl.ds(1, NR)], loc_sem.at[1])
    copy_w = pltpu.make_async_copy(w_hbm, w_v, loc_sem.at[2])
    copy_act.start()
    copy_cot.start()
    copy_w.start()

    barrier = pltpu.get_barrier_semaphore()

    def signal(device):
        pl.semaphore_signal(barrier, inc=1, device_id=device, device_id_type=MESH)

    for d in range(1, 16):
        signal(in_plane((plane + d) % 16))
    for d in range(1, 8):
        signal(in_row((xc + d) % 8))
    for device in (
        (span, above), (span, below), (before, above), (before, below), (after, above), (after, below)
    ):
        signal(device)

    def remote(src, dst, send, recv, device):
        return pltpu.make_async_remote_copy(
            src_ref=src, dst_ref=dst, send_sem=send, recv_sem=recv, device_id=device, device_id_type=MESH
        )

    def fold(v):
        return v.reshape(-1, 8, C).sum(axis=0)

    copy_act.wait()

    def local_sums(i, carry):
        one, two = carry
        v = act_v[i // NR, i % NR].astype(F32)
        return one + fold(v), two + fold(v * v)

    zero8 = jnp.zeros((8, C), F32)
    one, two = lax.fori_loop(0, NF * NR, local_sums, (zero8, zero8))
    row = lax.broadcasted_iota(jnp.int32, (8, C), 0)

    def stacked(*sums):
        value = zero8
        for n, v in enumerate(sums):
            value = jnp.where(row == n, jnp.broadcast_to(v.sum(axis=0, keepdims=True), (8, C)), value)
        return value

    def plane_copy(n, peer, slot):
        return remote(stat.at[n, 0], arb.at[n, slot], arb_s.at[n, peer], arb_r.at[n, slot], in_plane(peer))

    def row_copy(n, peer, slot):
        return remote(stat.at[n, 1], ara.at[n, slot], ara_s.at[n, peer], ara_r.at[n, slot], in_row(peer))

    def reduce_start(n, value):
        stat[n, 0] = value
        arb[n, plane] = value
        for d in range(1, 16):
            plane_copy(n, (plane + d) % 16, plane).start()

    def reduce_middle(n):
        for d in range(1, 16):
            plane_copy(n, (plane + d) % 16, (plane + d) % 16).wait_recv()
        value = arb[n].sum(axis=0)
        stat[n, 1] = value
        ara[n, xc] = value
        for d in range(1, 8):
            row_copy(n, (xc + d) % 8, xc).start()

    def reduce_end(n):
        for d in range(1, 8):
            row_copy(n, (xc + d) % 8, (xc + d) % 8).wait_recv()
        return ara[n].sum(axis=0)

    def reduce_drain(n):
        for d in range(1, 16):
            plane_copy(n, (plane + d) % 16, plane).wait_send()
        for d in range(1, 8):
            row_copy(n, (xc + d) % 8, xc).wait_send()

    pl.semaphore_wait(barrier, 28)

    halo = [
        remote(cot_hbm.at[:, 0], grad_v.at[pl.ds(0, NF), NR + 1], halo_s.at[0], halo_r.at[0], (span, above)),
        remote(cot_hbm.at[:, NR - 1], grad_v.at[pl.ds(0, NF), 0], halo_s.at[1], halo_r.at[1], (span, below)),
        remote(cot_hbm.at[0], grad_v.at[NF, pl.ds(1, NR)], halo_s.at[2], halo_r.at[2], (before, slab)),
        remote(cot_hbm.at[pl.ds(0, 2), 0], grad_v.at[pl.ds(NF, 2), NR + 1], halo_s.at[3], halo_r.at[3], (before, above)),
        remote(cot_hbm.at[pl.ds(0, 2), NR - 1], grad_v.at[pl.ds(NF, 2), 0], halo_s.at[4], halo_r.at[4], (before, below)),
        remote(cot_hbm.at[1], grad_v.at[NF + 1, pl.ds(1, NR)], halo_s.at[5], halo_r.at[5], (before, slab)),
    ]
    halo[0].start()
    halo[1].start()
    reduce_start(0, stacked(one, two))
    for h in halo[2:]:
        h.start()

    copy_cot.wait()

    def bias_local(i, carry):
        return carry + fold(grad_v[i // NR, 1 + i % NR].astype(F32))

    bias = lax.fori_loop(0, NF * NR, bias_local, zero8)

    def clear_rows(frames):
        @pl.when(slab == 0)
        def _():
            for f in frames:
                grad_v[f, 0] = jnp.zeros((W, C), BF16)

        @pl.when(slab == 15)
        def _():
            for f in frames:
                grad_v[f, NR + 1] = jnp.zeros((W, C), BF16)

    def shifted_sum(o):
        o = o.reshape(-1, W, 3 * C)
        pixel = lax.broadcasted_iota(jnp.int32, (1, W, C), 1)
        left = pltpu.roll(o[:, :, :C], W - 1, 1)
        right = pltpu.roll(o[:, :, 2 * C :], 1, 1)
        return o[:, :, C : 2 * C] + jnp.where(pixel < W - 1, left, 0.0) + jnp.where(pixel > 0, right, 0.0)

    def act_grad(t, taps, add):
        rhs = jnp.concatenate([w_v[a * 3 + b] for a in taps for b in range(3)], axis=1)
        half = NR // 2

        def part(i, _):
            r = i * half
            lhs = jnp.concatenate(
                [
                    grad_v[t + 2 - a, pl.ds(r + 2 - b, half)].reshape(half * W, C)
                    for a in taps
                    for b in range(3)
                ],
                axis=1,
            )
            o = shifted_sum(lax.dot_general(lhs, rhs, NT_DIMS, preferred_element_type=F32))
            if add:
                o = o + ag_v[t, pl.ds(r, half)]
            ag_v[t, pl.ds(r, half)] = o
            return 0

        lax.fori_loop(0, 2, part, 0)

    copy_w.wait()
    halo[0].wait_recv()
    halo[1].wait_recv()
    clear_rows(range(NF))
    act_grad(0, (2, 1, 0), False)
    reduce_middle(0)
    act_grad(1, (2, 1, 0), False)
    act_grad(2, (2, 1), False)
    act_grad(3, (2,), False)

    sums = group_sum(reduce_end(0))
    mean = sums[0:1] / MEMBERS
    variance = sums[1:2] / MEMBERS - mean * mean
    inv = lax.rsqrt(variance + 1e-06)
    gain, shift = gain_ref[...], shift_ref[...]

    def activate(i, _):
        t, r = i // NR, i % NR
        normed = (act_v[t, r].astype(F32) - mean) * inv
        scaled = normed * gain + shift
        sigma = jax.nn.sigmoid(scaled)
        dv_v[t, r] = sigma * (1.0 + scaled * (1.0 - sigma))
        turned = (scaled * sigma).T
        pixel = lax.broadcasted_iota(jnp.int32, (C, W), 1)
        at_v[t, r, 0:C] = jnp.where(pixel > 0, pltpu.roll(turned, 1, 1), 0.0).astype(BF16)
        at_v[t, r, C : 2 * C] = turned.astype(BF16)
        at_v[t, r, 2 * C : 3 * C] = jnp.where(pixel < W - 1, pltpu.roll(turned, W - 1, 1), 0.0).astype(BF16)
        return 0

    lax.fori_loop(0, NF * NR, activate, 0)

    def weight_part(a, frames, fresh):
        def one_frame(t):
            lhs = jnp.concatenate([at_v[t, r] for r in range(NR)], axis=1)
            rhs = jnp.concatenate(
                [grad_v[t + 2 - a, 2 - b : 2 - b + NR].reshape(ROWS, C) for b in range(3)], axis=1
            )
            return jnp.dot(lhs, rhs, preferred_element_type=F32)

        def put(o, add):
            for b in range(3):
                v = o[:, b * C : (b + 1) * C].reshape(3, C, C)
                if add:
                    v = v + wacc[a, 3 * b : 3 * b + 3]
                wacc[a, 3 * b : 3 * b + 3] = v

        first, last = frames
        if fresh:
            put(one_frame(first), False)
            first += 1

        def step(t, _):
            put(one_frame(t), True)
            return 0

        if first < last:
            lax.fori_loop(first, last, step, 0)

    half0 = core * 64
    mine0 = half0 + x * 16
    twin = in_row(xc + 1 - 2 * core)

    def rows(ref, a, start, size):
        return ref.at[a, :, pl.ds(pl.multiple_of(start, 16), size)]

    def x_peer(k):
        return in_row(k * 2 + core)

    def core_copy(a):
        return remote(rows(wacc, a, 64 - half0, 64), rs_core.at[a], c_s.at[a], c_r.at[a], twin)

    def axis_copy(a, k, slot):
        return remote(
            rows(wacc, a, half0 + k * 16, 16), rs_axis.at[a, slot], x_s.at[a, k], x_r.at[a, slot], x_peer(k)
        )

    def piece_copy(a, p, slot):
        return remote(rs_own.at[a, p], rs_plane.at[a, slot], p_s.at[a, p], p_r.at[a, slot], in_plane(p))

    def tile(a, p):
        return wout.at[a, p, pl.ds(pl.multiple_of(mine0, 16), 16)]

    def tile_copy(a, p, owner):
        return remote(tile(a, owner), tile(a, owner), gp_s.at[a, p], gp_r.at[a, owner], in_plane(p))

    def gather_axis(a, k, owner):
        part = rows(wout, a, half0 + owner * 16, 16)
        return remote(part, part, gx_s.at[a, k], gx_r.at[a, owner], x_peer(k))

    def gather_core(a, start):
        part = rows(wout, a, start, 64)
        return remote(part, part, gc_s.at[a], gc_r.at[a], twin)

    def s0(a):
        core_copy(a).start()

    def s1(a):
        core_copy(a).wait_recv()
        here = pl.ds(pl.multiple_of(half0, 16), 64)
        wacc[a, :, here] = wacc[a, :, here] + rs_core[a]
        for d in range(1, 4):
            axis_copy(a, (x + d) % 4, x).start()

    def s2(a):
        for d in range(1, 4):
            axis_copy(a, (x + d) % 4, (x + d) % 4).wait_recv()
        rs_axis[a, x] = wacc[a, :, pl.ds(pl.multiple_of(mine0, 16), 16)]
        rs_own[a] = rs_axis[a].sum(axis=0)
        for d in range(1, 16):
            p = (plane + d) % 16

            @pl.when(p < 9)
            def _(p=p):
                piece_copy(a, p, plane).start()

    def s3(a):
        @pl.when(plane < 9)
        def _():
            for d in range(1, 16):
                piece_copy(a, plane, (plane + d) % 16).wait_recv()
            rs_plane[a, plane] = rs_own[a, plane]
            total = rs_plane[a].sum(axis=0) * SCALE
            wout[a, plane, pl.ds(pl.multiple_of(mine0, 16), 16)] = total.astype(BF16)
            for d in range(1, 16):
                tile_copy(a, (plane + d) % 16, plane).start()

    def s4(a):
        for p in range(9):

            @pl.when(plane != p)
            def _(p=p):
                tile_copy(a, p, p).wait_recv()

        for d in range(1, 4):
            gather_axis(a, (x + d) % 4, x).start()

    def s5(a):
        for d in range(1, 4):
            gather_axis(a, (x + d) % 4, (x + d) % 4).wait_recv()
        gather_core(a, half0).start()

    def s6(a):
        gather_core(a, 64 - half0).wait_recv()

    def drain(a):
        core_copy(a).wait_send()
        for d in range(1, 4):
            axis_copy(a, (x + d) % 4, x).wait_send()
            gather_axis(a, (x + d) % 4, x).wait_send()
        for d in range(1, 16):
            p = (plane + d) % 16

            @pl.when(p < 9)
            def _(p=p):
                piece_copy(a, p, plane).wait_send()

        @pl.when(plane < 9)
        def _():
            for d in range(1, 16):
                tile_copy(a, (plane + d) % 16, plane).wait_send()

        gather_core(a, half0).wait_send()

    weight_part(2, (0, 4), True)
    s0(2)
    weight_part(1, (0, 3), True)
    s1(2)
    weight_part(0, (0, 2), True)
    s2(2)

    for h in halo[2:]:
        h.wait_recv()
    clear_rows((NF, NF + 1))

    @pl.when(span == 7)
    def _():
        def clear(i, _):
            grad_v[NF + i // (NR + 2), i % (NR + 2)] = jnp.zeros((W, C), BF16)
            return 0

        lax.fori_loop(0, 2 * (NR + 2), clear, 0)

    weight_part(1, (3, 4), False)
    s0(1)
    weight_part(0, (2, 4), False)
    s0(0)
    s1(1)
    s3(2)
    act_grad(2, (0,), True)
    s1(0)
    s2(1)
    act_grad(3, (1, 0), True)
    s2(0)

    def finish(i, carry):
        t, r = i // NR, i % NR
        normed = (act_v[t, r].astype(F32) - mean) * inv
        pre = ag_v[t, r] * dv_v[t, r]
        ag_v[t, r] = pre
        return carry[0] + fold(pre * normed), carry[1] + fold(pre)

    gain_sum, shift_sum = lax.fori_loop(0, NF * NR, finish, (zero8, zero8))
    reduce_start(1, stacked(gain_sum, shift_sum, bias))
    s3(1)
    s4(2)
    s3(0)
    s5(2)
    reduce_middle(1)
    s4(1)
    s4(0)
    total = reduce_end(1)
    sums_ref[...] = total * SCALE
    means = group_sum(total * gain) / MEMBERS
    mean_two, mean_one = means[0:1], means[1:2]

    def result(i, _):
        t, r = i // NR, i % NR
        normed = (act_v[t, r].astype(F32) - mean) * inv
        outb[t, r] = (inv * (gain * ag_v[t, r] - mean_one - normed * mean_two)).astype(BF16)
        return 0

    lax.fori_loop(0, NF * NR, result, 0)
    copy_out = pltpu.make_async_copy(outb, out_hbm, out_sem.at[0])
    copy_out.start()
    s5(1)
    s5(0)
    s6(2)
    s6(1)
    s6(0)
    copy_weights = pltpu.make_async_copy(wout, wout_hbm, out_sem.at[1])
    copy_weights.start()
    for h in halo:
        h.wait_send()
    for n in range(2):
        reduce_drain(n)
    for a in range(3):
        drain(a)
    copy_out.wait()
    copy_weights.wait()


def body(activations, cotangent, conv_weight, norm_gain, norm_shift):
    anywhere = pl.BlockSpec(memory_space=pl.ANY)
    vmem = pl.BlockSpec(memory_space=pltpu.VMEM)
    dma = pltpu.SemaphoreType.DMA
    input_grad, weights, sums = pl.pallas_call(
        kernel,
        out_shape=(
            jax.ShapeDtypeStruct((NF, NR, W, C), BF16),
            jax.ShapeDtypeStruct((3, 9, C, C), BF16),
            jax.ShapeDtypeStruct((8, C), F32),
        ),
        in_specs=[anywhere, anywhere, anywhere, vmem, vmem],
        out_specs=(anywhere, anywhere, vmem),
        scratch_shapes=[
            pltpu.VMEM((NF, NR, W, C), BF16),
            pltpu.VMEM((NF + 2, NR + 2, W, C), BF16),
            pltpu.VMEM((9, 3 * C, C), BF16),
            pltpu.VMEM((NF, NR, 3 * C, W), BF16),
            pltpu.VMEM((NF, NR, W, C), F32),
            pltpu.VMEM((NF, NR, W, C), F32),
            pltpu.VMEM((3, 9, C, C), F32),
            pltpu.VMEM((3, 9, 64, C), F32),
            pltpu.VMEM((3, 4, 9, 16, C), F32),
            pltpu.VMEM((3, 9, 16, C), F32),
            pltpu.VMEM((3, 16, 16, C), F32),
            pltpu.VMEM((3, 9, C, C), BF16),
            pltpu.VMEM((NF, NR, W, C), BF16),
            pltpu.VMEM((2, 2, 8, C), F32),
            pltpu.VMEM((2, 16, 8, C), F32),
            pltpu.VMEM((2, 8, 8, C), F32),
            dma((3,)), dma((2,)), dma((6,)), dma((6,)),
            dma((2, 16)), dma((2, 16)), dma((2, 8)), dma((2, 8)),
            dma((3,)), dma((3,)), dma((3, 4)), dma((3, 4)), dma((3, 9)), dma((3, 16)),
            dma((3, 16)), dma((3, 9)), dma((3, 4)), dma((3, 4)), dma((3,)), dma((3,)),
        ],
        compiler_params=pltpu.CompilerParams(
            collective_id=0, has_side_effects=True, vmem_limit_bytes=56 * 1024 * 1024
        ),
    )(
        activations,
        cotangent,
        conv_weight.reshape(9, 3 * C, C),
        norm_gain.reshape(1, C),
        norm_shift.reshape(1, C),
    )
    weight_grad = weights.astype(F32).reshape(3, 3, 3, C, C)
    return input_grad, weight_grad, sums[0], sums[1], sums[2]


def solution(mesh):
    placed = (P("span", "slab", None, None), P("span", "slab", None, None), P(), P(), P())
    return jax.shard_map(
        body,
        mesh=mesh,
        in_specs=placed,
        out_specs=(P("span", "slab", None, None), P(), P(), P(), P()),
        check_vma=False,
    )
```

time: 251 us -> 82.1 us (0.33)
  blocking collectives: 130 us -> 0 us
  Pallas kernels: 0 us -> 76.3 us
  local copies, waits for them, and re-layouts: 36.7 us -> 2.28 us
  other arithmetic: 25.9 us -> 2.58 us
  starting transfers between devices: 21 us -> 0 us
  matrix products: 18 us -> 0 us
  waiting for transfers between devices: 16.8 us -> 0 us
    psum x10 -> x0, blocking collectives: 79.7 us -> none  [by_axis(): return functools.reduce(lax.psum, axes, x)]
    pallas_call x0 -> x1, Pallas kernels: none -> 76.3 us  [body(): pl.pallas_call(kernel, out_shape=(jax.ShapeDtypeStruct((NF, NR, W, C), BF...]
    all_to_all x2 -> x0, blocking collectives: 50.7 us -> none  [the longest x1 30.3 us: sent_and_summed(): lax.all_to_all(tiles, axis, split_axis=0, concat_axis=0, tiled=True)]
    slice x7 -> x0, local copies, waits for them, and re-layouts: 18.8 us -> none  [the longest x4 16.7 us: tap_columns(): pieces = [window[:, :, begin:begin + col_count] for begin in col_starts]]
    dot_general x18 -> x0, matrix products: 18 us -> none  [the longest x9 9.27 us: body(): jnp.dot(grad_cols, stacked, preferred_element_type=jnp.float32)]
    ppermute x6 -> x0, waiting for transfers between devices: 16.8 us -> none  [the longest x2 9.02 us: passed_along(): lax.ppermute(value, axis, [(source, source + steps) for source in range(f...]
    ppermute x6 -> x0, starting transfers between devices: 15 us -> none  [the longest x2 7.09 us: padded_2(): before = lax.ppermute(last, axis, up)]
    concatenate x10 -> x0, other arithmetic: 13.1 us -> none  [the longest x5 6.93 us: tap_columns(): jnp.concatenate(pieces, axis=-1)]
  transfers between devices with their start and end apart: 7 -> 0, of which waited for: 3 -> 0; matrix products, arithmetic and copies ran while one was open for 5% -> 0% of each run, Pallas kernels for 0% -> 0%
where the time goes in v1:
time: 82.1 us; the launch traced here: 81.9 us
  Pallas kernels  76.3 us (93%)
  other arithmetic  2.58 us (3%)
  local copies, waits for them, and re-layouts  2.28 us (3%)
    pallas_call x1, Pallas kernels, body(): pl.pallas_call(kernel, out_shape=(jax.ShapeDtypeStruct((NF, NR, W, C), BF...  76.3 us
    reshape x1, other arithmetic, body(): weight_grad = weights.astype(F32).reshape(3, 3, 3, C, C)  2.58 us

profile of v1, /device:TPU:1, one launch (start us, length us, event | category | flops | bytes accessed | tf_op | source)
XLA Modules:
  0.0 81.9 jit_solution(13761849488702905977)
XLA Ops:
  0.6 76.3 %shard_map.92 = (bf16[4,8,128,128]{3,2,1,0:T(8,128)(2,1)}, bf16[3,9,128,128]{3,2,1,0:T(8,128)(2,1)}, f32[8,128]{1,0:T(8,128)}) custom-call(bf16[4,8,128,128]{3,2,1,0:T(8,128)(2,1)} %act_hbm.1, bf16[4,8,128,128]{3,2,1,0:T(8,128)(2,1)} %cot_hbm.1, bf16[9,384,128]{2,1,0:T(8,128)(2,1)} %bitcast.11, f32[1,128]{1,0:T(1,128)} %bitcast.13, f32[1,128]{1,0:T(1,128)} %bitcast.14), custom_call_target="tpu_custom_call" | custom-call | tf_op jit(solution)/shard_map/pallas_call | solution.py:434
  77.0 0.0 copy-start
  77.0 1.3 %slice_bitcast_fusion = (f32[128]{0:T(128)}, f32[128]{0:T(128)}, f32[128]{0:T(128)}) fusion(f32[8,128]{1,0:T(8,128)} %get-tuple-element.10), kind=kLoop, calls=%fused_computation | loop fusion | bytes 3072 | tf_op jit(solution)/shard_map/squeeze | solution.py:476
  78.3 2.6 %convert.1 = f32[3,3,3,128,128]{4,3,2,1,0:T(8,128)} convert(bf16[3,3,3,128,128]{4,3,2,1,0:T(8,128)(2,1)} %bitcast.12) | non-fusion elementwise | flops 442368 | bytes 2654208 | tf_op jit(solution)/shard_map/reshape | solution.py:475
  80.9 0.0 copy-done
  80.9 1.0 %copy.11 = bf16[4,8,128,128]{3,2,1,0:T(8,128)(2,1)} copy(bf16[4,8,128,128]{3,2,1,0:T(8,128)(2,1)S(1)} %copy-done) | data formatting | bytes 2097152
Async XLA Ops:
  77.0 3.9 %copy-start = (bf16[4,8,128,128]{3,2,1,0:T(8,128)(2,1)S(1)}, bf16[4,8,128,128]{3,2,1,0:T(8,128)(2,1)}, u32[]{:S(2)}) copy-start(bf16[4,8,128,128]{3,2,1,0:T(8,128)(2,1)} %get-tuple-element.19) | copy-start | bytes 3145732

commit v2 on v1

v2 whole, which is shorter than its diff:
```python
import jax
import jax.numpy as jnp
from jax import lax
from jax.experimental import pallas as pl
from jax.experimental.pallas import tpu as pltpu
from jax.sharding import PartitionSpec as P

MESH = pl.DeviceIdType.MESH
F32 = jnp.float32
BF16 = jnp.bfloat16
NF, NR, W, C = 4, 8, 128, 128
ROWS = NR * W
CELLS = 32 * 128 * 128
MEMBERS = CELLS * 4
SCALE = float(CELLS) ** -0.5
NT_DIMS = (((1,), (1,)), ((), ()))


def group_sum(v):
    lane = lax.broadcasted_iota(jnp.int32, v.shape, 1)
    v = v + jnp.where(lane % 2 == 0, pltpu.roll(v, C - 1, 1), pltpu.roll(v, 1, 1))
    return v + jnp.where(lane % 4 < 2, pltpu.roll(v, C - 2, 1), pltpu.roll(v, 2, 1))


def fold(v):
    return v.reshape(-1, 8, C).sum(axis=0)


def kernel(
    act_hbm, cot_hbm, w_hbm, gain_ref, shift_ref,
    out_hbm, wout_hbm, sums_ref,
    act_v, grad_v, w_v, at_v, ag_v, dv_v, wacc, rs_core, rs_axis, rs_own, rs_plane, wout, outb, stat, arb, ara, relay,
    loc_sem, out_sem, halo_s, halo_r, hop_s, hop_r, ar_s, ar_r,
    c_s, c_r, x_s, x_r, p_s, p_r, gp_s, gp_r, gx_s, gx_r, gc_s, gc_r,
):
    span, slab = lax.axis_index("span"), lax.axis_index("slab")
    z, y = span // 2, (span % 2) * 2 + slab // 8
    xc = slab % 8
    x, core = xc // 2, xc % 2

    def chip(cz, cy, cx, cc=core):
        return (cz * 2 + cy // 2, (cy % 2) * 8 + cx * 2 + cc)

    copies_act = [pltpu.make_async_copy(act_hbm.at[t], act_v.at[t], loc_sem.at[t]) for t in range(NF)]
    copy_cot = pltpu.make_async_copy(cot_hbm, grad_v.at[pl.ds(0, NF), pl.ds(1, NR)], loc_sem.at[NF])
    copy_w = pltpu.make_async_copy(w_hbm, w_v, loc_sem.at[NF + 1])
    for copy in copies_act:
        copy.start()
    copy_cot.start()
    copy_w.start()

    barrier = pltpu.get_barrier_semaphore()
    above = (span, (slab + 15) % 16)
    below = (span, (slab + 1) % 16)
    greeted = [above, below]
    for dz in range(4):
        for dy in range(4):
            for dx in range(4):
                if 0 in (dz, dy, dx) and (dz, dy, dx) != (0, 0, 0):
                    greeted.append(chip((z + dz) % 4, (y + dy) % 4, (x + dx) % 4))
    for dx in range(4):
        greeted.append(chip(z, y, (x + dx) % 4, 1 - core))
    for device in greeted:
        pl.semaphore_signal(barrier, inc=1, device_id=device, device_id_type=MESH)

    def remote(src, dst, send, recv, device):
        return pltpu.make_async_remote_copy(
            src_ref=src, dst_ref=dst, send_sem=send, recv_sem=recv, device_id=device, device_id_type=MESH
        )

    def take(ref, recv):
        remote(ref, ref, recv, recv, below).wait_recv()

    def sent(ref, send):
        remote(ref, ref, send, send, below).wait_send()

    zero8 = jnp.zeros((8, C), F32)
    one, two = zero8, zero8
    for t in range(NF):
        copies_act[t].wait()

        def local_sums(r, carry, t=t):
            v = act_v[t, r].astype(F32)
            return carry[0] + fold(v), carry[1] + fold(v * v)

        one, two = lax.fori_loop(0, NR, local_sums, (one, two), unroll=2)
    row = lax.broadcasted_iota(jnp.int32, (8, C), 0)

    def stacked(*sums):
        value = zero8
        for n, v in enumerate(sums):
            value = jnp.where(row == n, jnp.broadcast_to(v.sum(axis=0, keepdims=True), (8, C)), value)
        return value

    def in_yz(q):
        return chip(q // 4, q % 4, x)

    def in_row(j):
        return chip(z, y, j // 2, j % 2)

    yz = z * 4 + y

    def reduce_start(n, value):
        stat[n, 0] = value
        arb[n, yz] = value
        for d in range(1, 16):
            remote(stat.at[n, 0], arb.at[n, yz], ar_s.at[n, 0], ar_r.at[n, 0], in_yz((yz + d) % 16)).start()

    def reduce_middle(n):
        take(arb.at[n, pl.ds(0, 15)], ar_r.at[n, 0])
        value = arb[n].sum(axis=0)
        stat[n, 1] = value
        ara[n, xc] = value
        for d in range(1, 8):
            remote(stat.at[n, 1], ara.at[n, xc], ar_s.at[n, 1], ar_r.at[n, 1], in_row((xc + d) % 8)).start()

    def reduce_end(n):
        take(ara.at[n, pl.ds(0, 7)], ar_r.at[n, 1])
        return ara[n].sum(axis=0)

    def reduce_drain(n):
        sent(arb.at[n, pl.ds(0, 15)], ar_s.at[n, 0])
        sent(ara.at[n, pl.ds(0, 7)], ar_s.at[n, 1])

    pl.semaphore_wait(barrier, len(greeted))

    halo = [
        remote(cot_hbm.at[:, 0], grad_v.at[pl.ds(0, NF), NR + 1], halo_s.at[0], halo_r.at[0], above),
        remote(cot_hbm.at[:, NR - 1], grad_v.at[pl.ds(0, NF), 0], halo_s.at[1], halo_r.at[1], below),
        remote(grad_v.at[pl.ds(NF, 2), 1], grad_v.at[pl.ds(NF, 2), NR + 1], halo_s.at[2], halo_r.at[2], above),
        remote(grad_v.at[pl.ds(NF, 2), NR], grad_v.at[pl.ds(NF, 2), 0], halo_s.at[3], halo_r.at[3], below),
    ]
    up, down = (y + 1) % 4, (y + 3) % 4

    def earlier(cz, cy):
        return (cz + 3 + cy // 2) % 4

    first_to = (chip(z, up, x), chip(earlier(z, y), down, x))
    then_to = (chip(earlier(z, down), up, x), chip(z, down, x))
    quarter = NR // 2

    def first_hop(f, i):
        part = pl.ds(i * quarter, quarter)
        return remote(cot_hbm.at[f, part], relay.at[f, part], hop_s.at[0, f, i], hop_r.at[0, f, i], first_to[f])

    def second_hop(f, i):
        part = pl.ds(i * quarter, quarter)
        to = grad_v.at[NF + f, pl.ds(1 + i * quarter, quarter)]
        return remote(relay.at[f, part], to, hop_s.at[1, f, i], hop_r.at[1, f, i], then_to[f])

    def pass_on(i):
        for f in range(2):
            first_hop(f, i).wait_recv()
            second_hop(f, i).start()

    halo[0].start()
    halo[1].start()
    reduce_start(0, stacked(one, two))
    for i in range(2):
        for f in range(2):
            first_hop(f, i).start()

    copy_cot.wait()

    def bias_local(i, carry):
        return carry + fold(grad_v[i // NR, 1 + i % NR].astype(F32))

    bias = lax.fori_loop(0, NF * NR, bias_local, zero8, unroll=2)

    def clear_rows(frames):
        @pl.when(slab == 0)
        def _():
            for f in frames:
                grad_v[f, 0] = jnp.zeros((W, C), BF16)

        @pl.when(slab == 15)
        def _():
            for f in frames:
                grad_v[f, NR + 1] = jnp.zeros((W, C), BF16)

    def shifted_sum(o):
        o = o.reshape(-1, W, 3 * C)
        pixel = lax.broadcasted_iota(jnp.int32, (1, W, C), 1)
        left = pltpu.roll(o[:, :, :C], W - 1, 1)
        right = pltpu.roll(o[:, :, 2 * C :], 1, 1)
        return o[:, :, C : 2 * C] + jnp.where(pixel < W - 1, left, 0.0) + jnp.where(pixel > 0, right, 0.0)

    def act_grad(t, taps, add):
        rhs = jnp.concatenate([w_v[a * 3 + b] for a in taps for b in range(3)], axis=1)
        half = NR // 2

        def part(i, _):
            r = i * half
            lhs = jnp.concatenate(
                [
                    grad_v[t + 2 - a, pl.ds(r + 2 - b, half)].reshape(half * W, C)
                    for a in taps
                    for b in range(3)
                ],
                axis=1,
            )
            o = shifted_sum(lax.dot_general(lhs, rhs, NT_DIMS, preferred_element_type=F32))
            if add:
                o = o + ag_v[t, pl.ds(r, half)]
            ag_v[t, pl.ds(r, half)] = o
            return 0

        lax.fori_loop(0, 2, part, 0)

    copy_w.wait()
    halo[0].wait_recv()
    halo[1].wait_recv()
    clear_rows(range(NF))
    act_grad(0, (2, 1, 0), False)
    pass_on(0)
    reduce_middle(0)
    act_grad(1, (2, 1, 0), False)
    pass_on(1)

    sums = group_sum(reduce_end(0))
    mean = sums[0:1] / MEMBERS
    variance = sums[1:2] / MEMBERS - mean * mean
    inv = lax.rsqrt(variance + 1e-06)
    gain, shift = gain_ref[...], shift_ref[...]

    def activate(i, _):
        t, r = i // NR, i % NR
        normed = (act_v[t, r].astype(F32) - mean) * inv
        scaled = normed * gain + shift
        sigma = jax.nn.sigmoid(scaled)
        dv_v[t, r] = sigma * (1.0 + scaled * (1.0 - sigma))
        turned = (scaled * sigma).T
        pixel = lax.broadcasted_iota(jnp.int32, (C, W), 1)
        at_v[t, r, 0:C] = jnp.where(pixel > 0, pltpu.roll(turned, 1, 1), 0.0).astype(BF16)
        at_v[t, r, C : 2 * C] = turned.astype(BF16)
        at_v[t, r, 2 * C : 3 * C] = jnp.where(pixel < W - 1, pltpu.roll(turned, W - 1, 1), 0.0).astype(BF16)
        return 0

    lax.fori_loop(0, NF * NR, activate, 0, unroll=2)

    def weight_part(taps, frames, fresh):
        def step(t, add):
            lhs = jnp.concatenate([at_v[t, r] for r in range(NR)], axis=1)
            rhs = jnp.concatenate(
                [grad_v[t + 2 - a, 2 - b : 2 - b + NR].reshape(ROWS, C) for a in taps for b in range(3)], axis=1
            )
            o = jnp.dot(lhs, rhs, preferred_element_type=F32)
            n = 0
            for a in taps:
                for b in range(3):
                    v = o[:, n * C : (n + 1) * C].reshape(3, C, C)
                    at = pl.ds((2 - a) * 3, 3)
                    wacc[b, at] = v + wacc[b, at] if add else v
                    n += 1

        def again(t, _):
            step(t, True)
            return 0

        first, last = frames
        if fresh:
            step(first, False)
            first += 1
        lax.fori_loop(first, last, again, 0)

    half0 = core * 64
    twin = chip(z, y, x, 1 - core)
    place = (x, y, z)
    plane = (z * 4 + y, z * 4 + x, y * 4 + x)
    phases = (pl.ds(0, 3), pl.ds(3, 6))

    def on_axis(b, k):
        return (chip(z, y, k), chip(z, k, x), chip(k, y, x))[b]

    def on_plane(b, q):
        u, v = q // 4, q % 4
        return (chip(u, v, x), chip(u, y, v), chip(z, u, v))[b]

    def span_of(start, size):
        return pl.ds(pl.multiple_of(start, 16), size)

    def core_send(n):
        src = wacc.at[:, phases[n], span_of(64 - half0, 64)]
        remote(src, rs_core.at[:, phases[n]], c_s.at[n], c_r.at[n], twin).start()

    def axis_send(n):
        take(rs_core.at[:, phases[n]], c_r.at[n])
        here = span_of(half0, 64)
        for b in range(3):
            wacc[b, phases[n], here] = wacc[b, phases[n], here] + rs_core[b, phases[n]]
            for d in range(1, 4):
                k = (place[b] + d) % 4
                src = wacc.at[b, phases[n], span_of(half0 + k * 16, 16)]
                to = rs_axis.at[b, place[b], phases[n]]
                remote(src, to, x_s.at[n, b], x_r.at[n, b], on_axis(b, k)).start()

    def plane_send(b):
        for n in range(2):
            take(rs_axis.at[b, pl.ds(0, 3), phases[n]], x_r.at[n, b])
        rs_axis[b, place[b]] = wacc[b, :, span_of(half0 + place[b] * 16, 16)]
        rs_own[b] = rs_axis[b].sum(axis=0)
        for d in range(1, 16):
            p = (plane[b] + d) % 16

            @pl.when(p < 9)
            def _(p=p):
                remote(rs_own.at[b, p], rs_plane.at[b, plane[b]], p_s.at[b], p_r.at[b], on_plane(b, p)).start()

    def tile(b, p):
        return wout.at[b, p, span_of(half0 + place[b] * 16, 16)]

    def owner_sum(b):
        @pl.when(plane[b] < 9)
        def _():
            take(rs_plane.at[b, pl.ds(0, 15)], p_r.at[b])
            rs_plane[b, plane[b]] = rs_own[b, plane[b]]
            total = rs_plane[b].sum(axis=0) * SCALE
            wout[b, plane[b], span_of(half0 + place[b] * 16, 16)] = total.astype(BF16)
            for d in range(1, 16):
                p = (plane[b] + d) % 16
                remote(tile(b, plane[b]), tile(b, plane[b]), gp_s.at[b], gp_r.at[b], on_plane(b, p)).start()

    def gather_axis(b):
        tiles = wout.at[b, :, span_of(half0 + place[b] * 16, 16)]

        @pl.when(plane[b] < 9)
        def _():
            take(wout.at[b, pl.ds(0, 8), pl.ds(0, 16)], gp_r.at[b])

        @pl.when(plane[b] >= 9)
        def _():
            take(wout.at[b, :, pl.ds(0, 16)], gp_r.at[b])

        for d in range(1, 4):
            remote(tiles, tiles, gx_s.at[b], gx_r.at[b], on_axis(b, (place[b] + d) % 4)).start()

    def gather_core(b):
        take(wout.at[b, :, pl.ds(0, 48)], gx_r.at[b])
        part = wout.at[b, :, span_of(half0, 64)]
        remote(part, part, gc_s.at[b], gc_r.at[b], twin).start()

    def drain(b):
        for n in range(2):
            sent(rs_axis.at[b, pl.ds(0, 3), phases[n]], x_s.at[n, b])

        @pl.when(plane[b] < 9)
        def _():
            sent(rs_own.at[b, pl.ds(0, 8)], p_s.at[b])
            sent(wout.at[b, pl.ds(0, 5), pl.ds(0, 48)], gp_s.at[b])

        @pl.when(plane[b] >= 9)
        def _():
            sent(rs_own.at[b], p_s.at[b])

        sent(wout.at[b, :, pl.ds(0, 48)], gx_s.at[b])
        sent(wout.at[b, :, pl.ds(0, 64)], gc_s.at[b])

    weight_part((2,), (0, NF), True)
    core_send(0)
    weight_part((1, 0), (0, 2), True)
    axis_send(0)

    for i in range(2):
        for f in range(2):
            second_hop(f, i).wait_recv()
    halo[2].start()
    halo[3].start()
    act_grad(2, (2, 1), False)
    act_grad(3, (2,), False)
    halo[2].wait_recv()
    halo[3].wait_recv()
    halo[2].wait_send()
    halo[3].wait_send()
    clear_rows((NF, NF + 1))

    @pl.when(span == 7)
    def _():
        def clear(i, _):
            grad_v[NF + i // (NR + 2), i % (NR + 2)] = jnp.zeros((W, C), BF16)
            return 0

        lax.fori_loop(0, 2 * (NR + 2), clear, 0)

    weight_part((1, 0), (2, NF), False)
    core_send(1)
    act_grad(2, (0,), True)
    axis_send(1)
    act_grad(3, (1, 0), True)

    def finish(i, carry):
        t, r = i // NR, i % NR
        normed = (act_v[t, r].astype(F32) - mean) * inv
        pre = ag_v[t, r] * dv_v[t, r]
        ag_v[t, r] = pre
        return carry[0] + fold(pre * normed), carry[1] + fold(pre)

    gain_sum, shift_sum = lax.fori_loop(0, NF * NR, finish, (zero8, zero8), unroll=2)
    reduce_start(1, stacked(gain_sum, shift_sum, bias))
    for b in range(3):
        plane_send(b)
    reduce_middle(1)
    for b in range(3):
        owner_sum(b)
    total = reduce_end(1)
    sums_ref[...] = total * SCALE
    means = group_sum(total * gain) / MEMBERS
    mean_two, mean_one = means[0:1], means[1:2]

    def result(i, _):
        t, r = i // NR, i % NR
        normed = (act_v[t, r].astype(F32) - mean) * inv
        outb[t, r] = (inv * (gain * ag_v[t, r] - mean_one - normed * mean_two)).astype(BF16)
        return 0

    lax.fori_loop(0, NF * NR, result, 0, unroll=2)
    copy_out = pltpu.make_async_copy(outb, out_hbm, out_sem.at[0])
    copy_out.start()
    for b in range(3):
        gather_axis(b)
    for b in range(3):
        gather_core(b)
    for n in range(2):
        reduce_drain(n)
        sent(rs_core.at[:, phases[n]], c_s.at[n])
        halo[n].wait_send()
        for f in range(2):
            first_hop(f, n).wait_send()
            second_hop(f, n).wait_send()
    for b in range(3):
        take(wout.at[b, :, pl.ds(0, 64)], gc_r.at[b])
    copy_weights = pltpu.make_async_copy(wout, wout_hbm, out_sem.at[1])
    copy_weights.start()
    for b in range(3):
        drain(b)
    copy_out.wait()
    copy_weights.wait()


def write_out(in_hbm, w_hbm, sums_ref, out_hbm, wout_hbm, gain_ref, shift_ref, bias_ref, in_v, w_v, wide, sem):
    copy_w = pltpu.make_async_copy(w_hbm, w_v, sem.at[0])
    copy_in = pltpu.make_async_copy(in_hbm, in_v, sem.at[1])
    copy_w.start()
    copy_in.start()
    gain_ref[...] = sums_ref[0:1]
    shift_ref[...] = sums_ref[1:2]
    bias_ref[...] = sums_ref[2:3]
    copy_w.wait()
    outs = []
    for a in range(3):
        for b in range(3):
            wide[a, b] = w_v[b, (2 - a) * 3 : (3 - a) * 3].astype(F32)
        outs.append(pltpu.make_async_copy(wide.at[a], wout_hbm.at[a], sem.at[2 + a]))
        outs[-1].start()
    copy_in.wait()
    outs.append(pltpu.make_async_copy(in_v, out_hbm, sem.at[5]))
    outs[-1].start()
    for copy in outs:
        copy.wait()


def body(activations, cotangent, conv_weight, norm_gain, norm_shift):
    anywhere = pl.BlockSpec(memory_space=pl.ANY)
    vmem = pl.BlockSpec(memory_space=pltpu.VMEM)
    dma = pltpu.SemaphoreType.DMA
    input_grad, weights, sums = pl.pallas_call(
        kernel,
        out_shape=(
            jax.ShapeDtypeStruct((NF, NR, W, C), BF16),
            jax.ShapeDtypeStruct((3, 9, C, C), BF16),
            jax.ShapeDtypeStruct((8, C), F32),
        ),
        in_specs=[anywhere, anywhere, anywhere, vmem, vmem],
        out_specs=(anywhere, anywhere, vmem),
        scratch_shapes=[
            pltpu.VMEM((NF, NR, W, C), BF16),
            pltpu.VMEM((NF + 2, NR + 2, W, C), BF16),
            pltpu.VMEM((9, 3 * C, C), BF16),
            pltpu.VMEM((NF, NR, 3 * C, W), BF16),
            pltpu.VMEM((NF, NR, W, C), F32),
            pltpu.VMEM((NF, NR, W, C), F32),
            pltpu.VMEM((3, 9, C, C), F32),
            pltpu.VMEM((3, 9, 64, C), F32),
            pltpu.VMEM((3, 4, 9, 16, C), F32),
            pltpu.VMEM((3, 9, 16, C), F32),
            pltpu.VMEM((3, 16, 16, C), F32),
            pltpu.VMEM((3, 9, C, C), BF16),
            pltpu.VMEM((NF, NR, W, C), BF16),
            pltpu.VMEM((2, 2, 8, C), F32),
            pltpu.VMEM((2, 16, 8, C), F32),
            pltpu.VMEM((2, 8, 8, C), F32),
            pltpu.VMEM((2, NR, W, C), BF16),
            dma((6,)), dma((2,)), dma((4,)), dma((4,)), dma((2, 2, 2)), dma((2, 2, 2)), dma((2, 2)), dma((2, 2)),
            dma((2,)), dma((2,)), dma((2, 3)), dma((2, 3)), dma((3,)), dma((3,)),
            dma((3,)), dma((3,)), dma((3,)), dma((3,)), dma((3,)), dma((3,)),
        ],
        compiler_params=pltpu.CompilerParams(
            collective_id=0, has_side_effects=True, vmem_limit_bytes=56 * 1024 * 1024
        ),
    )(
        activations,
        cotangent,
        conv_weight.reshape(9, 3 * C, C),
        norm_gain.reshape(1, C),
        norm_shift.reshape(1, C),
    )
    per_channel = jax.ShapeDtypeStruct((1, C), F32)
    input_grad, weight_grad, gain_grad, shift_grad, bias_grad = pl.pallas_call(
        write_out,
        out_shape=(
            jax.ShapeDtypeStruct((NF, NR, W, C), BF16),
            jax.ShapeDtypeStruct((3, 3, 3, C, C), F32),
            per_channel,
            per_channel,
            per_channel,
        ),
        in_specs=[anywhere, anywhere, vmem],
        out_specs=(anywhere, anywhere, vmem, vmem, vmem),
        scratch_shapes=[
            pltpu.VMEM((NF, NR, W, C), BF16),
            pltpu.VMEM((3, 9, C, C), BF16),
            pltpu.VMEM((3, 3, 3, C, C), F32),
            dma((6,)),
        ],
        compiler_params=pltpu.CompilerParams(vmem_limit_bytes=62 * 1024 * 1024),
    )(input_grad, weights, sums)
    return input_grad, weight_grad, gain_grad.reshape(C), shift_grad.reshape(C), bias_grad.reshape(C)


def solution(mesh):
    placed = (P("span", "slab", None, None), P("span", "slab", None, None), P(), P(), P())
    return jax.shard_map(
        body,
        mesh=mesh,
        in_specs=placed,
        out_specs=(P("span", "slab", None, None), P(), P(), P(), P()),
        check_vma=False,
    )
```

time: 82.1 us -> 63.3 us (0.77)
  Pallas kernels: 76.3 us -> 62.5 us
  other arithmetic: 2.58 us -> 0 us
  local copies, waits for them, and re-layouts: 2.28 us -> 0 us
    pallas_call x1, Pallas kernels: 76.3 us -> 58.5 us  [body(): pl.pallas_call(kernel, out_shape=(jax.ShapeDtypeStruct((NF, NR, W, C), BF...]
    pallas_call x0 -> x1, Pallas kernels: none -> 4.01 us  [body(): pl.pallas_call(write_out, out_shape=(jax.ShapeDtypeStruct((NF, NR, W, C),...]
    reshape x1 -> x0, other arithmetic: 2.58 us -> none  [body(): weight_grad = weights.astype(F32).reshape(3, 3, 3, C, C)]
    squeeze x1 -> x0, local copies, waits for them, and re-layouts: 1.31 us -> none  [body(): return (input_grad, weight_grad, sums[0], sums[1], sums[2])]
    unnamed x3 -> x0, local copies, waits for them, and re-layouts: 0.97 us -> none
where the time goes in v2:
time: 63.3 us; the launch traced here: 63.1 us
  Pallas kernels  62.5 us (99%)
  between operations  0.64 us (1%)
    pallas_call x1, Pallas kernels, body(): pl.pallas_call(kernel, out_shape=(jax.ShapeDtypeStruct((NF, NR, W, C), BF...  58.5 us
    pallas_call x1, Pallas kernels, body(): pl.pallas_call(write_out, out_shape=(jax.ShapeDtypeStruct((NF, NR, W, C),...  4.01 us

profile of v2, /device:TPU:1, one launch (start us, length us, event | category | flops | bytes accessed | tf_op | source)
XLA Modules:
  0.0 63.1 jit_solution(3552491879980186000)
XLA Ops:
  0.6 58.5 %shard_map.92 = (bf16[4,8,128,128]{3,2,1,0:T(8,128)(2,1)}, bf16[3,9,128,128]{3,2,1,0:T(8,128)(2,1)}, f32[8,128]{1,0:T(8,128)}) custom-call(bf16[4,8,128,128]{3,2,1,0:T(8,128)(2,1)} %act_hbm.1, bf16[4,8,128,128]{3,2,1,0:T(8,128)(2,1)} %cot_hbm.1, bf16[9,384,128]{2,1,0:T(8,128)(2,1)} %bitcast.6, f32[1,128]{1,0:T(1,128)} %bitcast.7, f32[1,128]{1,0:T(1,128)} %bitcast.8), custom_call_target="tpu_custom_call" | custom-call | tf_op jit(solution)/shard_map/pallas_call | solution.py:465
  59.1 4.0 %shard_map.93 = (bf16[4,8,128,128]{3,2,1,0:T(8,128)(2,1)}, f32[3,3,3,128,128]{4,3,2,1,0:T(8,128)}, f32[1,128]{1,0:T(1,128)}, f32[1,128]{1,0:T(1,128)}, f32[1,128]{1,0:T(1,128)}) custom-call(bf16[4,8,128,128]{3,2,1,0:T(8,128)(2,1)} %get-tuple-element.13.in_hbm, bf16[3,9,128,128]{3,2,1,0:T(8,128)(2,1)} %get-tuple-element.14.w_hbm, ...), custom_call_target="tpu_custom_call" | custom-call | tf_op jit(solution)/shard_map/pallas_call | solution.py:507

commit v3 on v2

--- a/solution.py
+++ b/solution.py
@@ -28,9 +28,9 @@
 
 def kernel(
     act_hbm, cot_hbm, w_hbm, gain_ref, shift_ref,
-    out_hbm, wout_hbm, sums_ref,
-    act_v, grad_v, w_v, at_v, ag_v, dv_v, wacc, rs_core, rs_axis, rs_own, rs_plane, wout, outb, stat, arb, ara, relay,
-    loc_sem, out_sem, halo_s, halo_r, hop_s, hop_r, ar_s, ar_r,
+    outb, wout, sums_ref,
+    act_v, grad_v, w_v, at_v, ag_v, dv_v, wacc, rs_core, rs_axis, rs_own, rs_plane, stat, arb, ara, relay,
+    loc_sem, halo_s, halo_r, hop_s, hop_r, ar_s, ar_r,
     c_s, c_r, x_s, x_r, p_s, p_r, gp_s, gp_r, gx_s, gx_r, gc_s, gc_r,
 ):
     span, slab = lax.axis_index("span"), lax.axis_index("slab")
@@ -102,25 +102,25 @@
 
     def reduce_start(n, value):
         stat[n, 0] = value
+        ara[n, xc] = value
+        for d in range(1, 8):
+            remote(stat.at[n, 0], ara.at[n, xc], ar_s.at[n, 0], ar_r.at[n, 0], in_row((xc + d) % 8)).start()
+
+    def reduce_middle(n):
+        take(ara.at[n, pl.ds(0, 7)], ar_r.at[n, 0])
+        value = ara[n].sum(axis=0)
+        stat[n, 1] = value
         arb[n, yz] = value
         for d in range(1, 16):
-            remote(stat.at[n, 0], arb.at[n, yz], ar_s.at[n, 0], ar_r.at[n, 0], in_yz((yz + d) % 16)).start()
-
-    def reduce_middle(n):
-        take(arb.at[n, pl.ds(0, 15)], ar_r.at[n, 0])
-        value = arb[n].sum(axis=0)
-        stat[n, 1] = value
-        ara[n, xc] = value
-        for d in range(1, 8):
-            remote(stat.at[n, 1], ara.at[n, xc], ar_s.at[n, 1], ar_r.at[n, 1], in_row((xc + d) % 8)).start()
+            remote(stat.at[n, 1], arb.at[n, yz], ar_s.at[n, 1], ar_r.at[n, 1], in_yz((yz + d) % 16)).start()
 
     def reduce_end(n):
-        take(ara.at[n, pl.ds(0, 7)], ar_r.at[n, 1])
-        return ara[n].sum(axis=0)
+        take(arb.at[n, pl.ds(0, 15)], ar_r.at[n, 1])
+        return arb[n].sum(axis=0)
 
     def reduce_drain(n):
-        sent(arb.at[n, pl.ds(0, 15)], ar_s.at[n, 0])
-        sent(ara.at[n, pl.ds(0, 7)], ar_s.at[n, 1])
+        sent(ara.at[n, pl.ds(0, 7)], ar_s.at[n, 0])
+        sent(arb.at[n, pl.ds(0, 15)], ar_s.at[n, 1])
 
     pl.semaphore_wait(barrier, len(greeted))
 
@@ -137,28 +137,38 @@
 
     first_to = (chip(z, up, x), chip(earlier(z, y), down, x))
     then_to = (chip(earlier(z, down), up, x), chip(z, down, x))
-    quarter = NR // 2
-
-    def first_hop(f, i):
-        part = pl.ds(i * quarter, quarter)
-        return remote(cot_hbm.at[f, part], relay.at[f, part], hop_s.at[0, f, i], hop_r.at[0, f, i], first_to[f])
-
-    def second_hop(f, i):
-        part = pl.ds(i * quarter, quarter)
-        to = grad_v.at[NF + f, pl.ds(1 + i * quarter, quarter)]
-        return remote(relay.at[f, part], to, hop_s.at[1, f, i], hop_r.at[1, f, i], then_to[f])
+    half = NR // 2
+    pieces = ((0, 0, half), (1, 0, 1), (1, 1, half - 1)), ((0, half, half), (1, NR - 1, 1), (1, half, half - 1))
+
+    def first_hop(d, i):
+        f, start, size = pieces[d][i]
+        to = relay.at[d, f, pl.ds(start - d * half, size)]
+        return remote(cot_hbm.at[f, pl.ds(start, size)], to, hop_s.at[0, d, i], hop_r.at[0, d, i], first_to[d])
+
+    def second_hop(d, i):
+        f, start, size = pieces[d][i]
+        src = relay.at[d, f, pl.ds(start - d * half, size)]
+        to = grad_v.at[NF + f, pl.ds(1 + start, size)]
+        return remote(src, to, hop_s.at[1, d, i], hop_r.at[1, d, i], then_to[d])
+
+    def send_first(i):
+        for d in range(2):
+            first_hop(d, i).start()
 
     def pass_on(i):
-        for f in range(2):
-            first_hop(f, i).wait_recv()
-            second_hop(f, i).start()
-
+        for d in range(2):
+            first_hop(d, i).wait_recv()
+            second_hop(d, i).start()
+
+    def arrive(i):
+        for d in range(2):
+            second_hop(d, i).wait_recv()
+
+    reduce_start(0, stacked(one, two))
     halo[0].start()
     halo[1].start()
-    reduce_start(0, stacked(one, two))
-    for i in range(2):
-        for f in range(2):
-            first_hop(f, i).start()
+    send_first(0)
+    send_first(1)
 
     copy_cot.wait()
 
@@ -185,10 +195,8 @@
         right = pltpu.roll(o[:, :, 2 * C :], 1, 1)
         return o[:, :, C : 2 * C] + jnp.where(pixel < W - 1, left, 0.0) + jnp.where(pixel > 0, right, 0.0)
 
-    def act_grad(t, taps, add):
+    def act_grad(t, taps, add, halves=(0, 2)):
         rhs = jnp.concatenate([w_v[a * 3 + b] for a in taps for b in range(3)], axis=1)
-        half = NR // 2
-
         def part(i, _):
             r = i * half
             lhs = jnp.concatenate(
@@ -205,17 +213,19 @@
             ag_v[t, pl.ds(r, half)] = o
             return 0
 
-        lax.fori_loop(0, 2, part, 0)
-
+        lax.fori_loop(*halves, part, 0)
+
+    reduce_middle(0)
+    send_first(2)
     copy_w.wait()
     halo[0].wait_recv()
     halo[1].wait_recv()
     clear_rows(range(NF))
     act_grad(0, (2, 1, 0), False)
     pass_on(0)
-    reduce_middle(0)
+    pass_on(1)
     act_grad(1, (2, 1, 0), False)
-    pass_on(1)
+    pass_on(2)
 
     sums = group_sum(reduce_end(0))
     mean = sums[0:1] / MEMBERS
@@ -236,7 +246,7 @@
         at_v[t, r, 2 * C : 3 * C] = jnp.where(pixel < W - 1, pltpu.roll(turned, W - 1, 1), 0.0).astype(BF16)
         return 0
 
-    lax.fori_loop(0, NF * NR, activate, 0, unroll=2)
+    lax.fori_loop(0, NF * NR, activate, 0, unroll=4)
 
     def weight_part(taps, frames, fresh):
         def step(t, add):
@@ -357,35 +367,36 @@
 
     weight_part((2,), (0, NF), True)
     core_send(0)
+    arrive(0)
+    arrive(1)
+    halo[2].start()
+    halo[3].start()
     weight_part((1, 0), (0, 2), True)
     axis_send(0)
-
-    for i in range(2):
-        for f in range(2):
-            second_hop(f, i).wait_recv()
-    halo[2].start()
-    halo[3].start()
-    act_grad(2, (2, 1), False)
-    act_grad(3, (2,), False)
     halo[2].wait_recv()
     halo[3].wait_recv()
     halo[2].wait_send()
     halo[3].wait_send()
     clear_rows((NF, NF + 1))
 
-    @pl.when(span == 7)
-    def _():
-        def clear(i, _):
-            grad_v[NF + i // (NR + 2), i % (NR + 2)] = jnp.zeros((W, C), BF16)
-            return 0
-
-        lax.fori_loop(0, 2 * (NR + 2), clear, 0)
-
-    weight_part((1, 0), (2, NF), False)
+    def clear_frame(f):
+        @pl.when(span == 7)
+        def _():
+            def clear(i, _):
+                grad_v[f, i] = jnp.zeros((W, C), BF16)
+                return 0
+
+            lax.fori_loop(0, NR + 2, clear, 0)
+
+    clear_frame(NF)
+    weight_part((1, 0), (2, 3), False)
+    arrive(2)
+    clear_frame(NF + 1)
+    weight_part((1, 0), (3, NF), False)
     core_send(1)
-    act_grad(2, (0,), True)
+    act_grad(3, (2, 1, 0), False)
     axis_send(1)
-    act_grad(3, (1, 0), True)
+    act_grad(2, (2, 1, 0), False)
 
     def finish(i, carry):
         t, r = i // NR, i % NR
@@ -413,8 +424,6 @@
         return 0
 
     lax.fori_loop(0, NF * NR, result, 0, unroll=2)
-    copy_out = pltpu.make_async_copy(outb, out_hbm, out_sem.at[0])
-    copy_out.start()
     for b in range(3):
         gather_axis(b)
     for b in range(3):
@@ -423,37 +432,27 @@
         reduce_drain(n)
         sent(rs_core.at[:, phases[n]], c_s.at[n])
         halo[n].wait_send()
-        for f in range(2):
-            first_hop(f, n).wait_send()
-            second_hop(f, n).wait_send()
+        for i in range(3):
+            first_hop(n, i).wait_send()
+            second_hop(n, i).wait_send()
     for b in range(3):
         take(wout.at[b, :, pl.ds(0, 64)], gc_r.at[b])
-    copy_weights = pltpu.make_async_copy(wout, wout_hbm, out_sem.at[1])
-    copy_weights.start()
     for b in range(3):
         drain(b)
-    copy_out.wait()
-    copy_weights.wait()
-
-
-def write_out(in_hbm, w_hbm, sums_ref, out_hbm, wout_hbm, gain_ref, shift_ref, bias_ref, in_v, w_v, wide, sem):
-    copy_w = pltpu.make_async_copy(w_hbm, w_v, sem.at[0])
-    copy_in = pltpu.make_async_copy(in_hbm, in_v, sem.at[1])
-    copy_w.start()
-    copy_in.start()
+
+
+def write_out(in_ref, w_ref, sums_ref, out_hbm, wout_hbm, gain_ref, shift_ref, bias_ref, wide, sem):
+    outs = []
+    for a in range(3):
+        for b in range(3):
+            wide[a, b] = w_ref[b, (2 - a) * 3 : (3 - a) * 3].astype(F32)
+        outs.append(pltpu.make_async_copy(wide.at[a], wout_hbm.at[a], sem.at[a]))
+        outs[-1].start()
+    outs.append(pltpu.make_async_copy(in_ref, out_hbm, sem.at[3]))
+    outs[-1].start()
     gain_ref[...] = sums_ref[0:1]
     shift_ref[...] = sums_ref[1:2]
     bias_ref[...] = sums_ref[2:3]
-    copy_w.wait()
-    outs = []
-    for a in range(3):
-        for b in range(3):
-            wide[a, b] = w_v[b, (2 - a) * 3 : (3 - a) * 3].astype(F32)
-        outs.append(pltpu.make_async_copy(wide.at[a], wout_hbm.at[a], sem.at[2 + a]))
-        outs[-1].start()
-    copy_in.wait()
-    outs.append(pltpu.make_async_copy(in_v, out_hbm, sem.at[5]))
-    outs[-1].start()
     for copy in outs:
         copy.wait()
 
@@ -465,12 +464,12 @@
     input_grad, weights, sums = pl.pallas_call(
         kernel,
         out_shape=(
-            jax.ShapeDtypeStruct((NF, NR, W, C), BF16),
-            jax.ShapeDtypeStruct((3, 9, C, C), BF16),
-            jax.ShapeDtypeStruct((8, C), F32),
+            pltpu.VMEM((NF, NR, W, C), BF16),
+            pltpu.VMEM((3, 9, C, C), BF16),
+            pltpu.VMEM((8, C), F32),
         ),
         in_specs=[anywhere, anywhere, anywhere, vmem, vmem],
-        out_specs=(anywhere, anywhere, vmem),
+        out_specs=(vmem, vmem, vmem),
         scratch_shapes=[
             pltpu.VMEM((NF, NR, W, C), BF16),
             pltpu.VMEM((NF + 2, NR + 2, W, C), BF16),
@@ -483,18 +482,16 @@
             pltpu.VMEM((3, 4, 9, 16, C), F32),
             pltpu.VMEM((3, 9, 16, C), F32),
             pltpu.VMEM((3, 16, 16, C), F32),
-            pltpu.VMEM((3, 9, C, C), BF16),
-            pltpu.VMEM((NF, NR, W, C), BF16),
             pltpu.VMEM((2, 2, 8, C), F32),
             pltpu.VMEM((2, 16, 8, C), F32),
             pltpu.VMEM((2, 8, 8, C), F32),
-            pltpu.VMEM((2, NR, W, C), BF16),
-            dma((6,)), dma((2,)), dma((4,)), dma((4,)), dma((2, 2, 2)), dma((2, 2, 2)), dma((2, 2)), dma((2, 2)),
+            pltpu.VMEM((2, 2, NR // 2, W, C), BF16),
+            dma((6,)), dma((4,)), dma((4,)), dma((2, 2, 3)), dma((2, 2, 3)), dma((2, 2)), dma((2, 2)),
             dma((2,)), dma((2,)), dma((2, 3)), dma((2, 3)), dma((3,)), dma((3,)),
             dma((3,)), dma((3,)), dma((3,)), dma((3,)), dma((3,)), dma((3,)),
         ],
         compiler_params=pltpu.CompilerParams(
-            collective_id=0, has_side_effects=True, vmem_limit_bytes=56 * 1024 * 1024
+            collective_id=0, has_side_effects=True, vmem_limit_bytes=65_000_000
         ),
     )(
         activations,
@@ -513,15 +510,10 @@
             per_channel,
             per_channel,
         ),
-        in_specs=[anywhere, anywhere, vmem],
+        in_specs=[vmem, vmem, vmem],
         out_specs=(anywhere, anywhere, vmem, vmem, vmem),
-        scratch_shapes=[
-            pltpu.VMEM((NF, NR, W, C), BF16),
-            pltpu.VMEM((3, 9, C, C), BF16),
-            pltpu.VMEM((3, 3, 3, C, C), F32),
-            dma((6,)),
-        ],
-        compiler_params=pltpu.CompilerParams(vmem_limit_bytes=62 * 1024 * 1024),
+        scratch_shapes=[pltpu.VMEM((3, 3, 3, C, C), F32), dma((4,))],
+        compiler_params=pltpu.CompilerParams(vmem_limit_bytes=16 * 1024 * 1024),
     )(input_grad, weights, sums)
     return input_grad, weight_grad, gain_grad.reshape(C), shift_grad.reshape(C), bias_grad.reshape(C)
 

time: 63.3 us -> 57.6 us (0.910)
  Pallas kernels: 62.5 us -> 56.8 us
    pallas_call x1, Pallas kernels: 58.5 us -> 54.7 us  [body(): pl.pallas_call(kernel, out_shape=(pltpu.VMEM((NF, NR, W, C), BF16), pltpu...]
    pallas_call x1, Pallas kernels: 4.01 us -> 2.15 us  [body(): pl.pallas_call(write_out, out_shape=(jax.ShapeDtypeStruct((NF, NR, W, C),...]
where the time goes in v3:
time: 57.6 us; the launch traced here: 57.4 us
  Pallas kernels  56.8 us (99%)
  between operations  0.64 us (1%)
    pallas_call x1, Pallas kernels, body(): pl.pallas_call(kernel, out_shape=(pltpu.VMEM((NF, NR, W, C), BF16), pltpu...  54.7 us
    pallas_call x1, Pallas kernels, body(): pl.pallas_call(write_out, out_shape=(jax.ShapeDtypeStruct((NF, NR, W, C),...  2.15 us

profile of v3, /device:TPU:1, one launch (start us, length us, event | category | flops | bytes accessed | tf_op | source)
XLA Modules:
  0.0 57.4 jit_solution(15238276355512205891)
XLA Ops:
  0.6 54.7 %shard_map.92 = (bf16[4,8,128,128]{3,2,1,0:T(8,128)(2,1)S(1)}, bf16[3,9,128,128]{3,2,1,0:T(8,128)(2,1)S(1)}, f32[8,128]{1,0:T(8,128)S(1)}) custom-call(bf16[4,8,128,128]{3,2,1,0:T(8,128)(2,1)} %act_hbm.1, bf16[4,8,128,128]{3,2,1,0:T(8,128)(2,1)} %cot_hbm.1, bf16[9,384,128]{2,1,0:T(8,128)(2,1)} %bitcast.6, f32[1,128]{1,0:T(1,128)} %bitcast.7, f32[1,128]{1,0:T(1,128)} %bitcast.8), custom_call_target="tpu_custom_call" | custom-call | tf_op jit(solution)/shard_map/pallas_call | solution.py:464
  55.3 2.1 %shard_map.93 = (bf16[4,8,128,128]{3,2,1,0:T(8,128)(2,1)}, f32[3,3,3,128,128]{4,3,2,1,0:T(8,128)}, f32[1,128]{1,0:T(1,128)}, f32[1,128]{1,0:T(1,128)}, f32[1,128]{1,0:T(1,128)}) custom-call(bf16[4,8,128,128]{3,2,1,0:T(8,128)(2,1)S(1)} %get-tuple-element.13.in_ref, bf16[3,9,128,128]{3,2,1,0:T(8,128)(2,1)S(1)} %get-tuple-element.14.w_ref, ...), custom_call_target="tpu_custom_call" | custom-call | tf_op jit(solution)/shard_map/pallas_call | solution.py:504

commit v4 on v3

v4 whole, which is shorter than its diff:
```python
import jax
import jax.numpy as jnp
from jax import lax
from jax.experimental import pallas as pl
from jax.experimental.pallas import tpu as pltpu
from jax.sharding import PartitionSpec as P

MESH = pl.DeviceIdType.MESH
F32 = jnp.float32
BF16 = jnp.bfloat16
NF, NR, W, C = 4, 8, 128, 128
ROWS = NR * W
CELLS = 32 * 128 * 128
MEMBERS = CELLS * 4
SCALE = float(CELLS) ** -0.5
SENT = 2 * NF * 64 + 2 * 2 * NR * 64 + 2 * (7 + 15) * 4 + 27 * 64 + 3 * 27 * 48 + 27 * 24 + 27 * 32
GROUPS = 3
NT_DIMS = (((1,), (1,)), ((), ()))


def group_sum(v):
    lane = lax.broadcasted_iota(jnp.int32, v.shape, 1)
    v = v + jnp.where(lane % 2 == 0, pltpu.roll(v, C - 1, 1), pltpu.roll(v, 1, 1))
    return v + jnp.where(lane % 4 < 2, pltpu.roll(v, C - 2, 1), pltpu.roll(v, 2, 1))


def fold(v):
    return v.reshape(-1, 8, C).sum(axis=0)


def kernel(
    act_hbm, cot_hbm, w_hbm, gain_ref, shift_ref,
    outb, wout, sums_ref,
    act_v, grad_v, w_v, at_v, ag_v, dv_v, wacc, rs_core, rs_axis, stat, arb, ara, relay,
    all_sent, loc_sem, send_sem, halo_r, hop_r, ar_r, c_r, x_r, y_r, z_r, gx_r, gc_r,
):
    span, slab = lax.axis_index("span"), lax.axis_index("slab")
    z, y = span // 2, (span % 2) * 2 + slab // 8
    xc = slab % 8
    x, core = xc // 2, xc % 2

    def chip(cz, cy, cx, cc=core):
        return (cz * 2 + cy // 2, (cy % 2) * 8 + cx * 2 + cc)

    copies_act = [pltpu.make_async_copy(act_hbm.at[t], act_v.at[t], loc_sem.at[t]) for t in range(NF)]
    copy_cot = pltpu.make_async_copy(cot_hbm, grad_v.at[pl.ds(0, NF), pl.ds(1, NR)], loc_sem.at[NF])
    copy_w = pltpu.make_async_copy(w_hbm, w_v, loc_sem.at[NF + 1])
    for copy in copies_act:
        copy.start()
    copy_cot.start()
    copy_w.start()

    barrier = pltpu.get_barrier_semaphore()
    above = (span, (slab + 15) % 16)
    below = (span, (slab + 1) % 16)
    greeted = [above, below]
    greeted += [chip((z + d // 4) % 4, (y + d % 4) % 4, x) for d in range(1, 16)]
    greeted += [chip(z, y, (x + d // 2) % 4, (core + d) % 2) for d in range(1, 8)]
    for device in greeted:
        pl.semaphore_signal(barrier, inc=1, device_id=device, device_id_type=MESH)

    def remote(src, dst, send, recv, device):
        return pltpu.make_async_remote_copy(
            src_ref=src, dst_ref=dst, send_sem=send, recv_sem=recv, device_id=device, device_id_type=MESH
        )

    def take(ref, recv):
        remote(ref, ref, recv, recv, below).wait_recv()

    def sent(ref, send):
        remote(ref, ref, send, send, below).wait_send()

    zero8 = jnp.zeros((8, C), F32)
    one, two = zero8, zero8
    for t in range(NF):
        copies_act[t].wait()

        def local_sums(r, carry, t=t):
            v = act_v[t, r].astype(F32)
            return carry[0] + fold(v), carry[1] + fold(v * v)

        one, two = lax.fori_loop(0, NR, local_sums, (one, two), unroll=2)
    row = lax.broadcasted_iota(jnp.int32, (4, C), 0)

    def stacked(*sums):
        value = jnp.zeros((4, C), F32)
        for n, v in enumerate(sums):
            value = jnp.where(row == n, jnp.broadcast_to(v.sum(axis=0, keepdims=True), (4, C)), value)
        return value

    def in_yz(q):
        return chip(q // 4, q % 4, x)

    def in_row(j):
        return chip(z, y, j // 2, j % 2)

    yz = z * 4 + y

    def reduce_start(n, value):
        stat[n, 0] = value
        ara[n, xc] = value
        for d in range(1, 8):
            remote(stat.at[n, 0], ara.at[n, xc], send_sem.at[0], ar_r.at[n, 0], in_row((xc + d) % 8)).start()

    def reduce_middle(n):
        take(ara.at[n, pl.ds(0, 7)], ar_r.at[n, 0])
        value = ara[n].sum(axis=0)
        stat[n, 1] = value
        arb[n, yz] = value
        for d in range(1, 16):
            remote(stat.at[n, 1], arb.at[n, yz], send_sem.at[0], ar_r.at[n, 1], in_yz((yz + d) % 16)).start()

    def reduce_end(n):
        take(arb.at[n, pl.ds(0, 15)], ar_r.at[n, 1])
        return arb[n].sum(axis=0)

    pl.semaphore_wait(barrier, len(greeted))

    halo = [
        remote(cot_hbm.at[:, 0], grad_v.at[pl.ds(0, NF), NR + 1], send_sem.at[0], halo_r.at[0], above),
        remote(cot_hbm.at[:, NR - 1], grad_v.at[pl.ds(0, NF), 0], send_sem.at[0], halo_r.at[1], below),
        remote(grad_v.at[NF, 1], grad_v.at[NF, NR + 1], send_sem.at[1], halo_r.at[2], above),
        remote(grad_v.at[NF, NR], grad_v.at[NF, 0], send_sem.at[2], halo_r.at[3], below),
        remote(grad_v.at[NF + 1, 1], grad_v.at[NF + 1, NR + 1], send_sem.at[3], halo_r.at[4], above),
        remote(grad_v.at[NF + 1, NR], grad_v.at[NF + 1, 0], send_sem.at[4], halo_r.at[5], below),
    ]
    up, down = (y + 1) % 4, (y + 3) % 4

    def earlier(cz, cy):
        return (cz + 3 + cy // 2) % 4

    first_to = (chip(z, up, x), chip(earlier(z, y), down, x))
    then_to = (chip(earlier(z, down), up, x), chip(z, down, x))
    half = NR // 2
    pieces = ((0, 0, half), (1, 0, 1), (1, 1, half - 1)), ((0, half, half), (1, NR - 1, 1), (1, half, half - 1))

    def first_hop(d, i):
        f, start, size = pieces[d][i]
        to = relay.at[d, f, pl.ds(start - d * half, size)]
        return remote(cot_hbm.at[f, pl.ds(start, size)], to, send_sem.at[0], hop_r.at[0, d, i], first_to[d])

    def second_hop(d, i):
        f, start, size = pieces[d][i]
        src = relay.at[d, f, pl.ds(start - d * half, size)]
        to = grad_v.at[NF + f, pl.ds(1 + start, size)]
        return remote(src, to, send_sem.at[0], hop_r.at[1, d, i], then_to[d])

    def send_first(i):
        for d in range(2):
            first_hop(d, i).start()

    def pass_on(i):
        for d in range(2):
            first_hop(d, i).wait_recv()
            second_hop(d, i).start()

    def arrive(i):
        for d in range(2):
            second_hop(d, i).wait_recv()

    reduce_start(0, stacked(one, two))
    halo[0].start()
    halo[1].start()
    send_first(0)
    send_first(1)

    copy_cot.wait()

    def bias_local(i, carry):
        return carry + fold(grad_v[i // NR, 1 + i % NR].astype(F32))

    bias = lax.fori_loop(0, NF * NR, bias_local, zero8, unroll=2)

    def clear_rows(frames):
        @pl.when(slab == 0)
        def _():
            for f in frames:
                grad_v[f, 0] = jnp.zeros((W, C), BF16)

        @pl.when(slab == 15)
        def _():
            for f in frames:
                grad_v[f, NR + 1] = jnp.zeros((W, C), BF16)

    def shifted_sum(o):
        o = o.reshape(-1, W, 3 * C)
        pixel = lax.broadcasted_iota(jnp.int32, (1, W, C), 1)
        left = pltpu.roll(o[:, :, :C], W - 1, 1)
        right = pltpu.roll(o[:, :, 2 * C :], 1, 1)
        return o[:, :, C : 2 * C] + jnp.where(pixel < W - 1, left, 0.0) + jnp.where(pixel > 0, right, 0.0)

    def act_grad(t, taps, add, parts=((0, 4), (4, 4))):
        rhs = jnp.concatenate([w_v[a * 3 + b] for a in taps for b in range(3)], axis=1)
        for r, n in parts:
            lhs = jnp.concatenate(
                [
                    grad_v[t + 2 - a, r + 2 - b : r + 2 - b + n].reshape(n * W, C)
                    for a in taps
                    for b in range(3)
                ],
                axis=1,
            )
            o = shifted_sum(lax.dot_general(lhs, rhs, NT_DIMS, preferred_element_type=F32))
            if add:
                o = o + ag_v[t, r : r + n]
            ag_v[t, r : r + n] = o

    inner, outer = ((2, 4),), ((0, 2), (6, 2))
    first, second = ((0, 4),), ((4, 4),)
    copy_w.wait()
    act_grad(0, (2, 1, 0), False, inner)
    act_grad(1, (2, 1, 0), False, inner)
    reduce_middle(0)
    send_first(2)
    halo[0].wait_recv()
    halo[1].wait_recv()
    clear_rows(range(NF))
    act_grad(0, (2, 1, 0), False, outer)
    pass_on(0)
    act_grad(1, (2, 1, 0), False, outer)
    pass_on(1)
    act_grad(3, (2,), False)
    sums = group_sum(reduce_end(0))
    mean = sums[0:1] / MEMBERS
    variance = sums[1:2] / MEMBERS - mean * mean
    inv = lax.rsqrt(variance + 1e-06)
    gain, shift = gain_ref[...], shift_ref[...]

    pixel = lax.broadcasted_iota(jnp.int32, (C, W), 1)

    def activate(t):
        for r in range(NR):
            normed = (act_v[t, r].astype(F32) - mean) * inv
            scaled = normed * gain + shift
            sigma = jax.nn.sigmoid(scaled)
            dv_v[t, r] = sigma * (1.0 + scaled * (1.0 - sigma))
            turned = (scaled * sigma).T
            at_v[t, r, 0:C] = jnp.where(pixel > 0, pltpu.roll(turned, 1, 1), 0.0).astype(BF16)
            at_v[t, r, C : 2 * C] = turned.astype(BF16)
            at_v[t, r, 2 * C : 3 * C] = jnp.where(pixel < W - 1, pltpu.roll(turned, W - 1, 1), 0.0).astype(BF16)

    def weight_part(taps, t, add):
        lhs = jnp.concatenate([at_v[t, r] for r in range(NR)], axis=1)
        rhs = jnp.concatenate(
            [grad_v[t + 2 - a, 2 - b : 2 - b + NR].reshape(ROWS, C) for a in taps for b in range(3)], axis=1
        )
        o = jnp.dot(lhs, rhs, preferred_element_type=F32)
        n = 0
        for a in taps:
            for b in range(3):
                v = o[:, n * C : (n + 1) * C].reshape(3, C, C)
                at = pl.ds((2 - a) * 3, 3)
                wacc[b, at] = v + wacc[b, at] if add else v
                n += 1

    half0 = core * 64
    twin = chip(z, y, x, 1 - core)
    place = (x, y, z)
    phases = (pl.ds(0, 3), pl.ds(3, 3), pl.ds(6, 3))
    groups = ((0, 3), (3, 6), (6, 9)) if GROUPS == 3 else ((0, 6), (6, 9))
    members = ((0,), (1,), (2,)) if GROUPS == 3 else ((0, 1), (2,))

    def on_axis(b, k):
        return (chip(z, y, k), chip(z, k, x), chip(k, y, x))[b]

    def span_of(start, size):
        return pl.ds(pl.multiple_of(start, 16), size)

    def core_send(n):
        src = wacc.at[:, phases[n], span_of(64 - half0, 64)]
        remote(src, rs_core.at[:, phases[n]], send_sem.at[0], c_r.at[n], twin).start()

    def axis_send(n):
        take(rs_core.at[:, phases[n]], c_r.at[n])
        here = span_of(half0, 64)
        for b in range(3):
            wacc[b, phases[n], here] = wacc[b, phases[n], here] + rs_core[b, phases[n]]
            for d in range(1, 4):
                k = (place[b] + d) % 4
                src = wacc.at[b, phases[n], span_of(half0 + k * 16, 16)]
                to = rs_axis.at[0, b, place[b], phases[n]]
                remote(src, to, send_sem.at[0], x_r.at[n, b], on_axis(b, k)).start()

    def mine(b):
        return span_of(half0 + place[b] * 16, 16)

    def exchange(k, g, b, value, recv):
        lo, hi = groups[g]
        axis = (b + k) % 3
        slot = rs_axis.at[k, b, place[axis], pl.ds(lo, hi - lo)]
        slot[...] = value
        for d in range(1, 4):
            remote(slot, slot, send_sem.at[0], recv.at[g, b], on_axis(axis, (place[axis] + d) % 4)).start()

    def along_second(g, b):
        lo, hi = groups[g]
        for n in members[g]:
            take(rs_axis.at[0, b, pl.ds(0, 3), phases[n]], x_r.at[n, b])
        rs_axis[0, b, place[b], pl.ds(lo, hi - lo)] = wacc[b, lo:hi, mine(b)]
        exchange(1, g, b, rs_axis[0, b, :, lo:hi].sum(axis=0), y_r)

    def along_third(g, b):
        lo, hi = groups[g]
        take(rs_axis.at[1, b, pl.ds(0, 3), pl.ds(lo, hi - lo)], y_r.at[g, b])
        exchange(2, g, b, rs_axis[1, b, :, lo:hi].sum(axis=0), z_r)

    def gather_axis(g, b):
        lo, hi = groups[g]
        take(rs_axis.at[2, b, pl.ds(0, 3), pl.ds(lo, hi - lo)], z_r.at[g, b])
        total = rs_axis[2, b, :, lo:hi].sum(axis=0) * SCALE
        wout[b, lo:hi, mine(b)] = total.astype(BF16)
        tiles = wout.at[b, pl.ds(lo, hi - lo), mine(b)]
        for d in range(1, 4):
            remote(tiles, tiles, send_sem.at[0], gx_r.at[g, b], on_axis(b, (place[b] + d) % 4)).start()

    def gather_core(g, b):
        lo, hi = groups[g]
        take(wout.at[b, pl.ds(lo, hi - lo), pl.ds(0, 48)], gx_r.at[g, b])
        part = wout.at[b, pl.ds(lo, hi - lo), span_of(half0, 64)]
        remote(part, part, send_sem.at[0], gc_r.at[g, b], twin).start()

    def complete(g, b):
        lo, hi = groups[g]
        take(wout.at[b, pl.ds(lo, hi - lo), pl.ds(0, 64)], gc_r.at[g, b])

    def clear_frame(f):
        @pl.when(span == 7)
        def _():
            def clear(i, _):
                grad_v[f, i] = jnp.zeros((W, C), BF16)
                return 0

            lax.fori_loop(0, NR + 2, clear, 0)

    activate(0)
    pass_on(2)
    weight_part((2,), 0, False)
    activate(1)
    weight_part((2,), 1, True)
    activate(2)
    arrive(0)
    halo[2].start()
    halo[3].start()
    weight_part((2,), 2, True)
    activate(3)
    weight_part((2,), 3, True)
    core_send(0)
    arrive(1)
    halo[4].start()
    halo[5].start()
    for t in range(3):
        weight_part((1,), t, t > 0)
    for t in range(2):
        weight_part((0,), t, t > 0)
    axis_send(0)
    for n in (2, 3):
        halo[n].wait_recv()
        halo[n].wait_send()
    clear_rows((NF,))
    clear_frame(NF)
    weight_part((1,), 3, True)
    core_send(1)
    weight_part((0,), 2, True)
    arrive(2)
    for n in (4, 5):
        halo[n].wait_recv()
        halo[n].wait_send()
    clear_rows((NF + 1,))
    clear_frame(NF + 1)
    weight_part((0,), 3, True)
    core_send(2)
    act_grad(3, (1, 0), True, first)
    axis_send(1)
    axis_send(2)
    act_grad(3, (1, 0), True, second)
    act_grad(2, (2, 1, 0), False, first)
    act_grad(2, (2, 1, 0), False, second)

    def finish(i, carry):
        t, r = i // NR, i % NR
        normed = (act_v[t, r].astype(F32) - mean) * inv
        pre = ag_v[t, r] * dv_v[t, r]
        ag_v[t, r] = pre
        return carry[0] + fold(pre * normed), carry[1] + fold(pre)

    gain_sum, shift_sum = lax.fori_loop(0, NF * NR, finish, (zero8, zero8), unroll=2)
    reduce_start(1, stacked(gain_sum, shift_sum, bias))
    for g in range(GROUPS):
        for b in range(3):
            along_second(g, b)
    reduce_middle(1)
    for g in range(GROUPS):
        for b in range(3):
            along_third(g, b)
    for g in range(GROUPS):
        for b in range(3):
            gather_axis(g, b)
    total = reduce_end(1)
    sums_ref[...] = total * SCALE
    means = group_sum(total * gain) / MEMBERS
    mean_two, mean_one = means[0:1], means[1:2]

    def result(i, _):
        t, r = i // NR, i % NR
        normed = (act_v[t, r].astype(F32) - mean) * inv
        outb[t, r] = (inv * (gain * ag_v[t, r] - mean_one - normed * mean_two)).astype(BF16)
        return 0

    lax.fori_loop(0, NF * NR, result, 0, unroll=2)
    for g in range(GROUPS):
        for b in range(3):
            gather_core(g, b)
    for g in range(GROUPS):
        for b in range(3):
            complete(g, b)
    sent(all_sent, send_sem.at[0])


def write_out(in_ref, w_ref, sums_ref, out_hbm, wout_hbm, gain_ref, shift_ref, bias_ref, wide, sem):
    outs = []
    for a in range(3):
        for b in range(3):
            wide[a, b] = w_ref[b, (2 - a) * 3 : (3 - a) * 3].astype(F32)
        outs.append(pltpu.make_async_copy(wide.at[a], wout_hbm.at[a], sem.at[a]))
        outs[-1].start()
    outs.append(pltpu.make_async_copy(in_ref, out_hbm, sem.at[3]))
    outs[-1].start()
    gain_ref[...] = sums_ref[0:1]
    shift_ref[...] = sums_ref[1:2]
    bias_ref[...] = sums_ref[2:3]
    for copy in outs:
        copy.wait()


def body(activations, cotangent, conv_weight, norm_gain, norm_shift):
    anywhere = pl.BlockSpec(memory_space=pl.ANY)
    vmem = pl.BlockSpec(memory_space=pltpu.VMEM)
    dma = pltpu.SemaphoreType.DMA
    input_grad, weights, sums = pl.pallas_call(
        kernel,
        out_shape=(
            pltpu.VMEM((NF, NR, W, C), BF16),
            pltpu.VMEM((3, 9, C, C), BF16),
            pltpu.VMEM((4, C), F32),
        ),
        in_specs=[anywhere, anywhere, anywhere, vmem, vmem],
        out_specs=(vmem, vmem, vmem),
        scratch_shapes=[
            pltpu.VMEM((NF, NR, W, C), BF16),
            pltpu.VMEM((NF + 2, NR + 2, W, C), BF16),
            pltpu.VMEM((9, 3 * C, C), BF16),
            pltpu.VMEM((NF, NR, 3 * C, W), BF16),
            pltpu.VMEM((NF, NR, W, C), F32),
            pltpu.VMEM((NF, NR, W, C), F32),
            pltpu.VMEM((3, 9, C, C), F32),
            pltpu.VMEM((3, 9, 64, C), F32),
            pltpu.VMEM((3, 3, 4, 9, 16, C), F32),
            pltpu.VMEM((2, 2, 4, C), F32),
            pltpu.VMEM((2, 16, 4, C), F32),
            pltpu.VMEM((2, 8, 4, C), F32),
            pltpu.VMEM((2, 2, NR // 2, W, C), BF16),
            pltpu.VMEM((SENT, C), F32),
            dma((6,)), dma((5,)), dma((6,)), dma((2, 2, 3)), dma((2, 2)), dma((3,)), dma((3, 3)),
            dma((GROUPS, 3)), dma((GROUPS, 3)), dma((GROUPS, 3)), dma((GROUPS, 3)),
        ],
        compiler_params=pltpu.CompilerParams(
            collective_id=0, has_side_effects=True, vmem_limit_bytes=65_000_000
        ),
    )(
        activations,
        cotangent,
        conv_weight.reshape(9, 3 * C, C),
        norm_gain.reshape(1, C),
        norm_shift.reshape(1, C),
    )
    per_channel = jax.ShapeDtypeStruct((1, C), F32)
    input_grad, weight_grad, gain_grad, shift_grad, bias_grad = pl.pallas_call(
        write_out,
        out_shape=(
            jax.ShapeDtypeStruct((NF, NR, W, C), BF16),
            jax.ShapeDtypeStruct((3, 3, 3, C, C), F32),
            per_channel,
            per_channel,
            per_channel,
        ),
        in_specs=[vmem, vmem, vmem],
        out_specs=(anywhere, anywhere, vmem, vmem, vmem),
        scratch_shapes=[pltpu.VMEM((3, 3, 3, C, C), F32), dma((4,))],
        compiler_params=pltpu.CompilerParams(vmem_limit_bytes=16 * 1024 * 1024),
    )(input_grad, weights, sums)
    return input_grad, weight_grad, gain_grad.reshape(C), shift_grad.reshape(C), bias_grad.reshape(C)


def solution(mesh):
    placed = (P("span", "slab", None, None), P("span", "slab", None, None), P(), P(), P())
    return jax.shard_map(
        body,
        mesh=mesh,
        in_specs=placed,
        out_specs=(P("span", "slab", None, None), P(), P(), P(), P()),
        check_vma=False,
    )
```

time: 57.6 us -> 50.2 us (0.87)
  Pallas kernels: 56.8 us -> 49.5 us
    pallas_call x1, Pallas kernels: 54.7 us -> 47.3 us  [body(): pl.pallas_call(kernel, out_shape=(pltpu.VMEM((NF, NR, W, C), BF16), pltpu...]
where the time goes in v4:
time: 50.2 us; the launch traced here: 50.1 us
  Pallas kernels  49.5 us (99%)
  between operations  0.64 us (1%)
    pallas_call x1, Pallas kernels, body(): pl.pallas_call(kernel, out_shape=(pltpu.VMEM((NF, NR, W, C), BF16), pltpu...  47.3 us
    pallas_call x1, Pallas kernels, body(): pl.pallas_call(write_out, out_shape=(jax.ShapeDtypeStruct((NF, NR, W, C),...  2.15 us

profile of v4, /device:TPU:1, one launch (start us, length us, event | category | flops | bytes accessed | tf_op | source)
XLA Modules:
  0.0 50.1 jit_solution(9381516943106632517)
XLA Ops:
  0.6 47.3 %shard_map.92 = (bf16[4,8,128,128]{3,2,1,0:T(8,128)(2,1)S(1)}, bf16[3,9,128,128]{3,2,1,0:T(8,128)(2,1)S(1)}, f32[4,128]{1,0:T(4,128)S(1)}) custom-call(bf16[4,8,128,128]{3,2,1,0:T(8,128)(2,1)} %act_hbm.1, bf16[4,8,128,128]{3,2,1,0:T(8,128)(2,1)} %cot_hbm.1, bf16[9,384,128]{2,1,0:T(8,128)(2,1)} %bitcast.6, f32[1,128]{1,0:T(1,128)} %bitcast.7, f32[1,128]{1,0:T(1,128)} %bitcast.8), custom_call_target="tpu_custom_call" | custom-call | tf_op jit(solution)/shard_map/pallas_call | solution.py:439
  48.0 2.1 %shard_map.93 = (bf16[4,8,128,128]{3,2,1,0:T(8,128)(2,1)}, f32[3,3,3,128,128]{4,3,2,1,0:T(8,128)}, f32[1,128]{1,0:T(1,128)}, f32[1,128]{1,0:T(1,128)}, f32[1,128]{1,0:T(1,128)}) custom-call(bf16[4,8,128,128]{3,2,1,0:T(8,128)(2,1)S(1)} %get-tuple-element.13.in_ref, bf16[3,9,128,128]{3,2,1,0:T(8,128)(2,1)S(1)} %get-tuple-element.14.w_ref, ...), custom_call_target="tpu_custom_call" | custom-call | tf_op jit(solution)/shard_map/pallas_call | solution.py:477

commit v5 on v4

--- a/solution.py
+++ b/solution.py
@@ -13,7 +13,7 @@
 CELLS = 32 * 128 * 128
 MEMBERS = CELLS * 4
 SCALE = float(CELLS) ** -0.5
-SENT = 2 * NF * 64 + 2 * 2 * NR * 64 + 2 * (7 + 15) * 4 + 27 * 64 + 3 * 27 * 48 + 27 * 24 + 27 * 32
+SENT = 2 * NF * 64 + 2 * NR * 64 + 2 * (7 + 15) * 4 + 27 * 64 + 3 * 27 * 48 + 27 * 24 + 27 * 32
 GROUPS = 3
 NT_DIMS = (((1,), (1,)), ((), ()))
 
@@ -30,9 +30,9 @@
 
 def kernel(
     act_hbm, cot_hbm, w_hbm, gain_ref, shift_ref,
-    outb, wout, sums_ref,
-    act_v, grad_v, w_v, at_v, ag_v, dv_v, wacc, rs_core, rs_axis, stat, arb, ara, relay,
-    all_sent, loc_sem, send_sem, halo_r, hop_r, ar_r, c_r, x_r, y_r, z_r, gx_r, gc_r,
+    outb, wide, sums_ref,
+    act_v, grad_v, w_v, at_v, ag_v, dv_v, wacc, rs_core, rs_axis, wout, stat, arb, ara,
+    all_sent, loc_sem, send_sem, halo_r, frame_r, ar_r, c_r, x_r, y_r, z_r, gx_r, gc_r,
 ):
     span, slab = lax.axis_index("span"), lax.axis_index("slab")
     z, y = span // 2, (span % 2) * 2 + slab // 8
@@ -124,45 +124,20 @@
         remote(grad_v.at[NF + 1, 1], grad_v.at[NF + 1, NR + 1], send_sem.at[3], halo_r.at[4], above),
         remote(grad_v.at[NF + 1, NR], grad_v.at[NF + 1, 0], send_sem.at[4], halo_r.at[5], below),
     ]
-    up, down = (y + 1) % 4, (y + 3) % 4
-
-    def earlier(cz, cy):
-        return (cz + 3 + cy // 2) % 4
-
-    first_to = (chip(z, up, x), chip(earlier(z, y), down, x))
-    then_to = (chip(earlier(z, down), up, x), chip(z, down, x))
+    before = ((span + 7) % 8, slab)
     half = NR // 2
-    pieces = ((0, 0, half), (1, 0, 1), (1, 1, half - 1)), ((0, half, half), (1, NR - 1, 1), (1, half, half - 1))
-
-    def first_hop(d, i):
-        f, start, size = pieces[d][i]
-        to = relay.at[d, f, pl.ds(start - d * half, size)]
-        return remote(cot_hbm.at[f, pl.ds(start, size)], to, send_sem.at[0], hop_r.at[0, d, i], first_to[d])
-
-    def second_hop(d, i):
-        f, start, size = pieces[d][i]
-        src = relay.at[d, f, pl.ds(start - d * half, size)]
+
+    def frame_send(f, start, size, n):
         to = grad_v.at[NF + f, pl.ds(1 + start, size)]
-        return remote(src, to, send_sem.at[0], hop_r.at[1, d, i], then_to[d])
-
-    def send_first(i):
-        for d in range(2):
-            first_hop(d, i).start()
-
-    def pass_on(i):
-        for d in range(2):
-            first_hop(d, i).wait_recv()
-            second_hop(d, i).start()
-
-    def arrive(i):
-        for d in range(2):
-            second_hop(d, i).wait_recv()
+        remote(cot_hbm.at[f, pl.ds(start, size)], to, send_sem.at[0], frame_r.at[n], before).start()
+
+    def arrive(n):
+        take(grad_v.at[NF, pl.ds(0, (NR, 2, NR - 2)[n])], frame_r.at[n])
 
     reduce_start(0, stacked(one, two))
     halo[0].start()
     halo[1].start()
-    send_first(0)
-    send_first(1)
+    frame_send(0, 0, half, 0)
 
     copy_cot.wait()
 
@@ -210,15 +185,18 @@
     copy_w.wait()
     act_grad(0, (2, 1, 0), False, inner)
     act_grad(1, (2, 1, 0), False, inner)
+    act_grad(2, (2, 1), False, inner)
     reduce_middle(0)
-    send_first(2)
+    frame_send(0, half, half, 0)
+    frame_send(1, 0, 1, 1)
+    frame_send(1, NR - 1, 1, 1)
+    frame_send(1, 1, NR - 2, 2)
     halo[0].wait_recv()
     halo[1].wait_recv()
     clear_rows(range(NF))
     act_grad(0, (2, 1, 0), False, outer)
-    pass_on(0)
     act_grad(1, (2, 1, 0), False, outer)
-    pass_on(1)
+    act_grad(2, (2, 1), False, outer)
     act_grad(3, (2,), False)
     sums = group_sum(reduce_end(0))
     mean = sums[0:1] / MEMBERS
@@ -239,26 +217,21 @@
             at_v[t, r, C : 2 * C] = turned.astype(BF16)
             at_v[t, r, 2 * C : 3 * C] = jnp.where(pixel < W - 1, pltpu.roll(turned, W - 1, 1), 0.0).astype(BF16)
 
-    def weight_part(taps, t, add):
+    def weight_part(a, t):
         lhs = jnp.concatenate([at_v[t, r] for r in range(NR)], axis=1)
         rhs = jnp.concatenate(
-            [grad_v[t + 2 - a, 2 - b : 2 - b + NR].reshape(ROWS, C) for a in taps for b in range(3)], axis=1
+            [grad_v[t + 2 - a, 2 - b : 2 - b + NR].reshape(ROWS, C) for b in range(3)], axis=1
         )
         o = jnp.dot(lhs, rhs, preferred_element_type=F32)
-        n = 0
-        for a in taps:
-            for b in range(3):
-                v = o[:, n * C : (n + 1) * C].reshape(3, C, C)
-                at = pl.ds((2 - a) * 3, 3)
-                wacc[b, at] = v + wacc[b, at] if add else v
-                n += 1
+        for b in range(3):
+            v = o[:, b * C : (b + 1) * C].reshape(3, C, C)
+            at = pl.ds((2 - a) * 3, 3)
+            wacc[b, at] = v + wacc[b, at] if t else v
 
     half0 = core * 64
     twin = chip(z, y, x, 1 - core)
     place = (x, y, z)
-    phases = (pl.ds(0, 3), pl.ds(3, 3), pl.ds(6, 3))
-    groups = ((0, 3), (3, 6), (6, 9)) if GROUPS == 3 else ((0, 6), (6, 9))
-    members = ((0,), (1,), (2,)) if GROUPS == 3 else ((0, 1), (2,))
+    groups = ((0, 3), (3, 6), (6, 9))
 
     def on_axis(b, k):
         return (chip(z, y, k), chip(z, k, x), chip(k, y, x))[b]
@@ -266,20 +239,22 @@
     def span_of(start, size):
         return pl.ds(pl.multiple_of(start, 16), size)
 
-    def core_send(n):
-        src = wacc.at[:, phases[n], span_of(64 - half0, 64)]
-        remote(src, rs_core.at[:, phases[n]], send_sem.at[0], c_r.at[n], twin).start()
-
-    def axis_send(n):
-        take(rs_core.at[:, phases[n]], c_r.at[n])
+    def core_send(g):
+        at = pl.ds(3 * g, 3)
+        src = wacc.at[:, at, span_of(64 - half0, 64)]
+        remote(src, rs_core.at[:, at], send_sem.at[0], c_r.at[g], twin).start()
+
+    def axis_send(g):
+        at = pl.ds(3 * g, 3)
+        take(rs_core.at[:, at], c_r.at[g])
         here = span_of(half0, 64)
         for b in range(3):
-            wacc[b, phases[n], here] = wacc[b, phases[n], here] + rs_core[b, phases[n]]
+            wacc[b, at, here] = wacc[b, at, here] + rs_core[b, at]
             for d in range(1, 4):
                 k = (place[b] + d) % 4
-                src = wacc.at[b, phases[n], span_of(half0 + k * 16, 16)]
-                to = rs_axis.at[0, b, place[b], phases[n]]
-                remote(src, to, send_sem.at[0], x_r.at[n, b], on_axis(b, k)).start()
+                src = wacc.at[b, at, span_of(half0 + k * 16, 16)]
+                to = rs_axis.at[0, b, place[b], at]
+                remote(src, to, send_sem.at[0], x_r.at[g, b], on_axis(b, k)).start()
 
     def mine(b):
         return span_of(half0 + place[b] * 16, 16)
@@ -294,8 +269,7 @@
 
     def along_second(g, b):
         lo, hi = groups[g]
-        for n in members[g]:
-            take(rs_axis.at[0, b, pl.ds(0, 3), phases[n]], x_r.at[n, b])
+        take(rs_axis.at[0, b, pl.ds(0, 3), pl.ds(lo, 3)], x_r.at[g, b])
         rs_axis[0, b, place[b], pl.ds(lo, hi - lo)] = wacc[b, lo:hi, mine(b)]
         exchange(1, g, b, rs_axis[0, b, :, lo:hi].sum(axis=0), y_r)
 
@@ -322,6 +296,12 @@
     def complete(g, b):
         lo, hi = groups[g]
         take(wout.at[b, pl.ds(lo, hi - lo), pl.ds(0, 64)], gc_r.at[g, b])
+        for j in range(lo, hi, 3):
+            wide[2 - j // 3, b] = wout[b, j : j + 3].astype(F32)
+
+    def each(stage, g):
+        for b in range(3):
+            stage(g, b)
 
     def clear_frame(f):
         @pl.when(span == 7)
@@ -332,49 +312,46 @@
 
             lax.fori_loop(0, NR + 2, clear, 0)
 
+    def outer_rows(n, f):
+        halo[n].wait_recv()
+        halo[n].wait_send()
+        halo[n + 1].wait_recv()
+        halo[n + 1].wait_send()
+        clear_rows((f,))
+        clear_frame(f)
+
     activate(0)
-    pass_on(2)
-    weight_part((2,), 0, False)
+    weight_part(2, 0)
     activate(1)
-    weight_part((2,), 1, True)
+    weight_part(2, 1)
     activate(2)
     arrive(0)
     halo[2].start()
     halo[3].start()
-    weight_part((2,), 2, True)
+    weight_part(2, 2)
     activate(3)
-    weight_part((2,), 3, True)
-    core_send(0)
     arrive(1)
     halo[4].start()
     halo[5].start()
+    weight_part(2, 3)
+    core_send(0)
     for t in range(3):
-        weight_part((1,), t, t > 0)
-    for t in range(2):
-        weight_part((0,), t, t > 0)
+        weight_part(1, t)
+    outer_rows(2, NF)
     axis_send(0)
-    for n in (2, 3):
-        halo[n].wait_recv()
-        halo[n].wait_send()
-    clear_rows((NF,))
-    clear_frame(NF)
-    weight_part((1,), 3, True)
+    weight_part(1, 3)
     core_send(1)
-    weight_part((0,), 2, True)
+    for t in range(3):
+        weight_part(0, t)
     arrive(2)
-    for n in (4, 5):
-        halo[n].wait_recv()
-        halo[n].wait_send()
-    clear_rows((NF + 1,))
-    clear_frame(NF + 1)
-    weight_part((0,), 3, True)
+    outer_rows(4, NF + 1)
+    axis_send(1)
+    weight_part(0, 3)
     core_send(2)
-    act_grad(3, (1, 0), True, first)
-    axis_send(1)
+    act_grad(3, (1, 0), True)
     axis_send(2)
-    act_grad(3, (1, 0), True, second)
-    act_grad(2, (2, 1, 0), False, first)
-    act_grad(2, (2, 1, 0), False, second)
+    each(along_second, 0)
+    act_grad(2, (0,), True)
 
     def finish(i, carry):
         t, r = i // NR, i % NR
@@ -385,16 +362,14 @@
 
     gain_sum, shift_sum = lax.fori_loop(0, NF * NR, finish, (zero8, zero8), unroll=2)
     reduce_start(1, stacked(gain_sum, shift_sum, bias))
-    for g in range(GROUPS):
-        for b in range(3):
-            along_second(g, b)
+    each(along_second, 1)
+    each(along_second, 2)
     reduce_middle(1)
-    for g in range(GROUPS):
-        for b in range(3):
-            along_third(g, b)
-    for g in range(GROUPS):
-        for b in range(3):
-            gather_axis(g, b)
+    each(along_third, 0)
+    each(along_third, 1)
+    each(along_third, 2)
+    each(gather_axis, 0)
+    each(gather_axis, 1)
     total = reduce_end(1)
     sums_ref[...] = total * SCALE
     means = group_sum(total * gain) / MEMBERS
@@ -407,28 +382,23 @@
         return 0
 
     lax.fori_loop(0, NF * NR, result, 0, unroll=2)
+    each(gather_axis, 2)
     for g in range(GROUPS):
-        for b in range(3):
-            gather_core(g, b)
+        each(gather_core, g)
     for g in range(GROUPS):
-        for b in range(3):
-            complete(g, b)
+        each(complete, g)
     sent(all_sent, send_sem.at[0])
 
 
-def write_out(in_ref, w_ref, sums_ref, out_hbm, wout_hbm, gain_ref, shift_ref, bias_ref, wide, sem):
-    outs = []
-    for a in range(3):
-        for b in range(3):
-            wide[a, b] = w_ref[b, (2 - a) * 3 : (3 - a) * 3].astype(F32)
-        outs.append(pltpu.make_async_copy(wide.at[a], wout_hbm.at[a], sem.at[a]))
-        outs[-1].start()
-    outs.append(pltpu.make_async_copy(in_ref, out_hbm, sem.at[3]))
-    outs[-1].start()
+def write_out(in_ref, w_ref, sums_ref, out_hbm, wout_hbm, gain_ref, shift_ref, bias_ref, sem):
+    copies = [pltpu.make_async_copy(w_ref.at[a], wout_hbm.at[a], sem.at[a]) for a in range(3)]
+    copies.append(pltpu.make_async_copy(in_ref, out_hbm, sem.at[3]))
+    for copy in copies:
+        copy.start()
     gain_ref[...] = sums_ref[0:1]
     shift_ref[...] = sums_ref[1:2]
     bias_ref[...] = sums_ref[2:3]
-    for copy in outs:
+    for copy in copies:
         copy.wait()
 
 
@@ -440,7 +410,7 @@
         kernel,
         out_shape=(
             pltpu.VMEM((NF, NR, W, C), BF16),
-            pltpu.VMEM((3, 9, C, C), BF16),
+            pltpu.VMEM((3, 3, 3, C, C), F32),
             pltpu.VMEM((4, C), F32),
         ),
         in_specs=[anywhere, anywhere, anywhere, vmem, vmem],
@@ -455,16 +425,16 @@
             pltpu.VMEM((3, 9, C, C), F32),
             pltpu.VMEM((3, 9, 64, C), F32),
             pltpu.VMEM((3, 3, 4, 9, 16, C), F32),
+            pltpu.VMEM((3, 9, C, C), BF16),
             pltpu.VMEM((2, 2, 4, C), F32),
             pltpu.VMEM((2, 16, 4, C), F32),
             pltpu.VMEM((2, 8, 4, C), F32),
-            pltpu.VMEM((2, 2, NR // 2, W, C), BF16),
             pltpu.VMEM((SENT, C), F32),
-            dma((6,)), dma((5,)), dma((6,)), dma((2, 2, 3)), dma((2, 2)), dma((3,)), dma((3, 3)),
+            dma((6,)), dma((5,)), dma((6,)), dma((3,)), dma((2, 2)), dma((3,)), dma((3, 3)),
             dma((GROUPS, 3)), dma((GROUPS, 3)), dma((GROUPS, 3)), dma((GROUPS, 3)),
         ],
         compiler_params=pltpu.CompilerParams(
-            collective_id=0, has_side_effects=True, vmem_limit_bytes=65_000_000
+            collective_id=0, has_side_effects=True, vmem_limit_bytes=64_100_000
         ),
     )(
         activations,
@@ -485,7 +455,7 @@
         ),
         in_specs=[vmem, vmem, vmem],
         out_specs=(anywhere, anywhere, vmem, vmem, vmem),
-        scratch_shapes=[pltpu.VMEM((3, 3, 3, C, C), F32), dma((4,))],
+        scratch_shapes=[dma((4,))],
         compiler_params=pltpu.CompilerParams(vmem_limit_bytes=16 * 1024 * 1024),
     )(input_grad, weights, sums)
     return input_grad, weight_grad, gain_grad.reshape(C), shift_grad.reshape(C), bias_grad.reshape(C)

time: 50.2 us -> 49.2 us (0.980)
  Pallas kernels: 49.5 us -> 48.4 us
    pallas_call x1, Pallas kernels: 47.3 us -> 46.3 us  [body(): pl.pallas_call(kernel, out_shape=(pltpu.VMEM((NF, NR, W, C), BF16), pltpu...]
where the time goes in v5:
time: 49.2 us; the launch traced here: 49 us
  Pallas kernels  48.4 us (98%)
  between operations  0.64 us (1%)
    pallas_call x1, Pallas kernels, body(): pl.pallas_call(kernel, out_shape=(pltpu.VMEM((NF, NR, W, C), BF16), pltpu...  46.3 us
    pallas_call x1, Pallas kernels, body(): pl.pallas_call(write_out, out_shape=(jax.ShapeDtypeStruct((NF, NR, W, C),...  2.11 us

profile of v5, /device:TPU:1, one launch (start us, length us, event | category | flops | bytes accessed | tf_op | source)
XLA Modules:
  0.0 49.0 jit_solution(9732748048340717270)
XLA Ops:
  0.6 46.3 %shard_map.92 = (bf16[4,8,128,128]{3,2,1,0:T(8,128)(2,1)S(1)}, f32[3,3,3,128,128]{4,3,2,1,0:T(8,128)S(1)}, f32[4,128]{1,0:T(4,128)S(1)}) custom-call(bf16[4,8,128,128]{3,2,1,0:T(8,128)(2,1)} %act_hbm.1, bf16[4,8,128,128]{3,2,1,0:T(8,128)(2,1)} %cot_hbm.1, bf16[9,384,128]{2,1,0:T(8,128)(2,1)} %bitcast.6, f32[1,128]{1,0:T(1,128)} %bitcast.7, f32[1,128]{1,0:T(1,128)} %bitcast.8), custom_call_target="tpu_custom_call" | custom-call | tf_op jit(solution)/shard_map/pallas_call | solution.py:409
  46.9 2.1 %shard_map.93 = (bf16[4,8,128,128]{3,2,1,0:T(8,128)(2,1)}, f32[3,3,3,128,128]{4,3,2,1,0:T(8,128)}, f32[1,128]{1,0:T(1,128)}, f32[1,128]{1,0:T(1,128)}, f32[1,128]{1,0:T(1,128)}) custom-call(bf16[4,8,128,128]{3,2,1,0:T(8,128)(2,1)S(1)} %get-tuple-element.13.in_ref, f32[3,3,3,128,128]{4,3,2,1,0:T(8,128)S(1)} %get-tuple-element.14.w_ref, ...), custom_call_target="tpu_custom_call" | custom-call | tf_op jit(solution)/shard_map/pallas_call | solution.py:447

commit v6 on v5

--- a/solution.py
+++ b/solution.py
@@ -13,7 +13,7 @@
 CELLS = 32 * 128 * 128
 MEMBERS = CELLS * 4
 SCALE = float(CELLS) ** -0.5
-SENT = 2 * NF * 64 + 2 * NR * 64 + 2 * (7 + 15) * 4 + 27 * 64 + 3 * 27 * 48 + 27 * 24 + 27 * 32
+SENT = 2 * NF * 64 + 2 * NR * 64 + 2 * (7 + 15) * 4 + 27 * 64 + 3 * 27 * 48 + 18 * 24 + 18 * 32 + 9 * 56
 GROUPS = 3
 NT_DIMS = (((1,), (1,)), ((), ()))
 
@@ -42,6 +42,20 @@
     def chip(cz, cy, cx, cc=core):
         return (cz * 2 + cy // 2, (cy % 2) * 8 + cx * 2 + cc)
 
+    barrier = pltpu.get_barrier_semaphore()
+    above = (span, (slab + 15) % 16)
+    below = (span, (slab + 1) % 16)
+    greeted = [chip(z, y, (x + d // 2) % 4, (core + d) % 2) for d in range(1, 8)]
+    greeted += [above, below]
+    greeted += [chip((z + d // 4) % 4, (y + d % 4) % 4, x) for d in range(1, 16)]
+    greeted += [chip(z, (y + d) % 4, x, 1 - core) for d in range(1, 4)]
+    greeted += [chip((z + d) % 4, y, x, 1 - core) for d in range(1, 4)]
+
+    def greet(devices):
+        for device in devices:
+            pl.semaphore_signal(barrier, inc=1, device_id=device, device_id_type=MESH)
+
+    greet(greeted[:7])
     copies_act = [pltpu.make_async_copy(act_hbm.at[t], act_v.at[t], loc_sem.at[t]) for t in range(NF)]
     copy_cot = pltpu.make_async_copy(cot_hbm, grad_v.at[pl.ds(0, NF), pl.ds(1, NR)], loc_sem.at[NF])
     copy_w = pltpu.make_async_copy(w_hbm, w_v, loc_sem.at[NF + 1])
@@ -49,15 +63,7 @@
         copy.start()
     copy_cot.start()
     copy_w.start()
-
-    barrier = pltpu.get_barrier_semaphore()
-    above = (span, (slab + 15) % 16)
-    below = (span, (slab + 1) % 16)
-    greeted = [above, below]
-    greeted += [chip((z + d // 4) % 4, (y + d % 4) % 4, x) for d in range(1, 16)]
-    greeted += [chip(z, y, (x + d // 2) % 4, (core + d) % 2) for d in range(1, 8)]
-    for device in greeted:
-        pl.semaphore_signal(barrier, inc=1, device_id=device, device_id_type=MESH)
+    greet(greeted[7:])
 
     def remote(src, dst, send, recv, device):
         return pltpu.make_async_remote_copy(
@@ -233,8 +239,8 @@
     place = (x, y, z)
     groups = ((0, 3), (3, 6), (6, 9))
 
-    def on_axis(b, k):
-        return (chip(z, y, k), chip(z, k, x), chip(k, y, x))[b]
+    def on_axis(b, k, cc=core):
+        return (chip(z, y, k, cc), chip(z, k, x, cc), chip(k, y, x, cc))[b]
 
     def span_of(start, size):
         return pl.ds(pl.multiple_of(start, 16), size)
@@ -284,8 +290,9 @@
         total = rs_axis[2, b, :, lo:hi].sum(axis=0) * SCALE
         wout[b, lo:hi, mine(b)] = total.astype(BF16)
         tiles = wout.at[b, pl.ds(lo, hi - lo), mine(b)]
-        for d in range(1, 4):
-            remote(tiles, tiles, send_sem.at[0], gx_r.at[g, b], on_axis(b, (place[b] + d) % 4)).start()
+        for d in range(1, 8) if g == 2 else (2, 4, 6):
+            to = on_axis(b, (place[b] + d // 2) % 4, (core + d) % 2)
+            remote(tiles, tiles, send_sem.at[0], gx_r.at[g, b], to).start()
 
     def gather_core(g, b):
         lo, hi = groups[g]
@@ -295,9 +302,11 @@
 
     def complete(g, b):
         lo, hi = groups[g]
-        take(wout.at[b, pl.ds(lo, hi - lo), pl.ds(0, 64)], gc_r.at[g, b])
-        for j in range(lo, hi, 3):
-            wide[2 - j // 3, b] = wout[b, j : j + 3].astype(F32)
+        if g == 2:
+            take(wout.at[b, pl.ds(lo, hi - lo), pl.ds(0, 112)], gx_r.at[g, b])
+        else:
+            take(wout.at[b, pl.ds(lo, hi - lo), pl.ds(0, 64)], gc_r.at[g, b])
+        wide[2 - g, b] = wout[b, lo:hi].astype(F32)
 
     def each(stage, g):
         for b in range(3):
@@ -337,17 +346,18 @@
     core_send(0)
     for t in range(3):
         weight_part(1, t)
+    for t in range(2):
+        weight_part(0, t)
+    axis_send(0)
     outer_rows(2, NF)
-    axis_send(0)
     weight_part(1, 3)
     core_send(1)
-    for t in range(3):
-        weight_part(0, t)
+    weight_part(0, 2)
     arrive(2)
     outer_rows(4, NF + 1)
-    axis_send(1)
     weight_part(0, 3)
     core_send(2)
+    axis_send(1)
     act_grad(3, (1, 0), True)
     axis_send(2)
     each(along_second, 0)
@@ -364,12 +374,13 @@
     reduce_start(1, stacked(gain_sum, shift_sum, bias))
     each(along_second, 1)
     each(along_second, 2)
-    reduce_middle(1)
     each(along_third, 0)
     each(along_third, 1)
+    reduce_middle(1)
     each(along_third, 2)
     each(gather_axis, 0)
     each(gather_axis, 1)
+    each(gather_axis, 2)
     total = reduce_end(1)
     sums_ref[...] = total * SCALE
     means = group_sum(total * gain) / MEMBERS
@@ -382,9 +393,8 @@
         return 0
 
     lax.fori_loop(0, NF * NR, result, 0, unroll=2)
-    each(gather_axis, 2)
-    for g in range(GROUPS):
-        each(gather_core, g)
+    each(gather_core, 0)
+    each(gather_core, 1)
     for g in range(GROUPS):
         each(complete, g)
     sent(all_sent, send_sem.at[0])
@@ -431,7 +441,7 @@
             pltpu.VMEM((2, 8, 4, C), F32),
             pltpu.VMEM((SENT, C), F32),
             dma((6,)), dma((5,)), dma((6,)), dma((3,)), dma((2, 2)), dma((3,)), dma((3, 3)),
-            dma((GROUPS, 3)), dma((GROUPS, 3)), dma((GROUPS, 3)), dma((GROUPS, 3)),
+            dma((GROUPS, 3)), dma((GROUPS, 3)), dma((GROUPS, 3)), dma((2, 3)),
         ],
         compiler_params=pltpu.CompilerParams(
             collective_id=0, has_side_effects=True, vmem_limit_bytes=64_100_000

time: 49.2 us -> 48.1 us (0.978)
  Pallas kernels: 48.4 us -> 47.3 us
    pallas_call x1, Pallas kernels: 46.3 us -> 45.2 us  [body(): pl.pallas_call(kernel, out_shape=(pltpu.VMEM((NF, NR, W, C), BF16), pltpu...]
where the time goes in v6:
time: 48.1 us; the launch traced here: 48 us
  Pallas kernels  47.3 us (98%)
  between operations  0.64 us (1%)
    pallas_call x1, Pallas kernels, body(): pl.pallas_call(kernel, out_shape=(pltpu.VMEM((NF, NR, W, C), BF16), pltpu...  45.2 us
    pallas_call x1, Pallas kernels, body(): pl.pallas_call(write_out, out_shape=(jax.ShapeDtypeStruct((NF, NR, W, C),...  2.11 us

profile of v6, /device:TPU:1, one launch (start us, length us, event | category | flops | bytes accessed | tf_op | source)
XLA Modules:
  0.0 48.0 jit_solution(9204885742023496693)
XLA Ops:
  0.6 45.2 %shard_map.92 = (bf16[4,8,128,128]{3,2,1,0:T(8,128)(2,1)S(1)}, f32[3,3,3,128,128]{4,3,2,1,0:T(8,128)S(1)}, f32[4,128]{1,0:T(4,128)S(1)}) custom-call(bf16[4,8,128,128]{3,2,1,0:T(8,128)(2,1)} %act_hbm.1, bf16[4,8,128,128]{3,2,1,0:T(8,128)(2,1)} %cot_hbm.1, bf16[9,384,128]{2,1,0:T(8,128)(2,1)} %bitcast.6, f32[1,128]{1,0:T(1,128)} %bitcast.7, f32[1,128]{1,0:T(1,128)} %bitcast.8), custom_call_target="tpu_custom_call" | custom-call | tf_op jit(solution)/shard_map/pallas_call | solution.py:419
  45.8 2.1 %shard_map.93 = (bf16[4,8,128,128]{3,2,1,0:T(8,128)(2,1)}, f32[3,3,3,128,128]{4,3,2,1,0:T(8,128)}, f32[1,128]{1,0:T(1,128)}, f32[1,128]{1,0:T(1,128)}, f32[1,128]{1,0:T(1,128)}) custom-call(bf16[4,8,128,128]{3,2,1,0:T(8,128)(2,1)S(1)} %get-tuple-element.13.in_ref, f32[3,3,3,128,128]{4,3,2,1,0:T(8,128)S(1)} %get-tuple-element.14.w_ref, ...), custom_call_target="tpu_custom_call" | custom-call | tf_op jit(solution)/shard_map/pallas_call | solution.py:457

commit v7 on v6

--- a/solution.py
+++ b/solution.py
@@ -29,9 +29,9 @@
 
 
 def kernel(
-    act_hbm, cot_hbm, w_hbm, gain_ref, shift_ref,
-    outb, wide, sums_ref,
-    act_v, grad_v, w_v, at_v, ag_v, dv_v, wacc, rs_core, rs_axis, wout, stat, arb, ara,
+    act_hbm, cot_hbm, w_hbm, gain_hbm, shift_hbm,
+    outb, wide, gain_out, shift_out, bias_out,
+    gain_v, shift_v, act_v, grad_v, w_v, at_v, ag_v, dv_v, wacc, rs_core, rs_axis, wout, stat, arb, ara,
     all_sent, loc_sem, send_sem, halo_r, frame_r, ar_r, c_r, x_r, y_r, z_r, gx_r, gc_r,
 ):
     span, slab = lax.axis_index("span"), lax.axis_index("slab")
@@ -59,10 +59,10 @@
     copies_act = [pltpu.make_async_copy(act_hbm.at[t], act_v.at[t], loc_sem.at[t]) for t in range(NF)]
     copy_cot = pltpu.make_async_copy(cot_hbm, grad_v.at[pl.ds(0, NF), pl.ds(1, NR)], loc_sem.at[NF])
     copy_w = pltpu.make_async_copy(w_hbm, w_v, loc_sem.at[NF + 1])
+    copy_gain = pltpu.make_async_copy(gain_hbm, gain_v, loc_sem.at[NF + 2])
+    copy_shift = pltpu.make_async_copy(shift_hbm, shift_v, loc_sem.at[NF + 3])
     for copy in copies_act:
         copy.start()
-    copy_cot.start()
-    copy_w.start()
     greet(greeted[7:])
 
     def remote(src, dst, send, recv, device):
@@ -80,6 +80,11 @@
     one, two = zero8, zero8
     for t in range(NF):
         copies_act[t].wait()
+        if t == NF - 2:
+            copy_cot.start()
+        if t == NF - 1:
+            for copy in (copy_w, copy_gain, copy_shift):
+                copy.start()
 
         def local_sums(r, carry, t=t):
             v = act_v[t, r].astype(F32)
@@ -208,7 +213,9 @@
     mean = sums[0:1] / MEMBERS
     variance = sums[1:2] / MEMBERS - mean * mean
     inv = lax.rsqrt(variance + 1e-06)
-    gain, shift = gain_ref[...], shift_ref[...]
+    copy_gain.wait()
+    copy_shift.wait()
+    gain, shift = gain_v[...], shift_v[...]
 
     pixel = lax.broadcasted_iota(jnp.int32, (C, W), 1)
 
@@ -358,9 +365,10 @@
     weight_part(0, 3)
     core_send(2)
     axis_send(1)
-    act_grad(3, (1, 0), True)
+    act_grad(3, (1, 0), True, first)
     axis_send(2)
     each(along_second, 0)
+    act_grad(3, (1, 0), True, second)
     act_grad(2, (0,), True)
 
     def finish(i, carry):
@@ -382,7 +390,10 @@
     each(gather_axis, 1)
     each(gather_axis, 2)
     total = reduce_end(1)
-    sums_ref[...] = total * SCALE
+    scaled_sums = total * SCALE
+    gain_out[...] = scaled_sums[0:1]
+    shift_out[...] = scaled_sums[1:2]
+    bias_out[...] = scaled_sums[2:3]
     means = group_sum(total * gain) / MEMBERS
     mean_two, mean_one = means[0:1], means[1:2]
 
@@ -400,14 +411,12 @@
     sent(all_sent, send_sem.at[0])
 
 
-def write_out(in_ref, w_ref, sums_ref, out_hbm, wout_hbm, gain_ref, shift_ref, bias_ref, sem):
-    copies = [pltpu.make_async_copy(w_ref.at[a], wout_hbm.at[a], sem.at[a]) for a in range(3)]
-    copies.append(pltpu.make_async_copy(in_ref, out_hbm, sem.at[3]))
+def write_out(in_ref, w_ref, gain_ref, shift_ref, bias_ref, out_hbm, wout_hbm, gain_hbm, shift_hbm, bias_hbm, sem):
+    pairs = [(w_ref.at[a], wout_hbm.at[a]) for a in range(3)]
+    pairs += [(in_ref, out_hbm), (gain_ref, gain_hbm), (shift_ref, shift_hbm), (bias_ref, bias_hbm)]
+    copies = [pltpu.make_async_copy(src, to, sem.at[n]) for n, (src, to) in enumerate(pairs)]
     for copy in copies:
         copy.start()
-    gain_ref[...] = sums_ref[0:1]
-    shift_ref[...] = sums_ref[1:2]
-    bias_ref[...] = sums_ref[2:3]
     for copy in copies:
         copy.wait()
 
@@ -416,16 +425,20 @@
     anywhere = pl.BlockSpec(memory_space=pl.ANY)
     vmem = pl.BlockSpec(memory_space=pltpu.VMEM)
     dma = pltpu.SemaphoreType.DMA
-    input_grad, weights, sums = pl.pallas_call(
+    results = pl.pallas_call(
         kernel,
         out_shape=(
             pltpu.VMEM((NF, NR, W, C), BF16),
             pltpu.VMEM((3, 3, 3, C, C), F32),
-            pltpu.VMEM((4, C), F32),
+            pltpu.VMEM((1, C), F32),
+            pltpu.VMEM((1, C), F32),
+            pltpu.VMEM((1, C), F32),
         ),
-        in_specs=[anywhere, anywhere, anywhere, vmem, vmem],
-        out_specs=(vmem, vmem, vmem),
+        in_specs=[anywhere] * 5,
+        out_specs=(vmem,) * 5,
         scratch_shapes=[
+            pltpu.VMEM((1, C), F32),
+            pltpu.VMEM((1, C), F32),
             pltpu.VMEM((NF, NR, W, C), BF16),
             pltpu.VMEM((NF + 2, NR + 2, W, C), BF16),
             pltpu.VMEM((9, 3 * C, C), BF16),
@@ -440,7 +453,7 @@
             pltpu.VMEM((2, 16, 4, C), F32),
             pltpu.VMEM((2, 8, 4, C), F32),
             pltpu.VMEM((SENT, C), F32),
-            dma((6,)), dma((5,)), dma((6,)), dma((3,)), dma((2, 2)), dma((3,)), dma((3, 3)),
+            dma((NF + 4,)), dma((5,)), dma((6,)), dma((3,)), dma((2, 2)), dma((3,)), dma((3, 3)),
             dma((GROUPS, 3)), dma((GROUPS, 3)), dma((GROUPS, 3)), dma((2, 3)),
         ],
         compiler_params=pltpu.CompilerParams(
@@ -463,11 +476,11 @@
             per_channel,
             per_channel,
         ),
-        in_specs=[vmem, vmem, vmem],
-        out_specs=(anywhere, anywhere, vmem, vmem, vmem),
-        scratch_shapes=[dma((4,))],
+        in_specs=[vmem] * 5,
+        out_specs=(anywhere,) * 5,
+        scratch_shapes=[dma((7,))],
         compiler_params=pltpu.CompilerParams(vmem_limit_bytes=16 * 1024 * 1024),
-    )(input_grad, weights, sums)
+    )(*results)
     return input_grad, weight_grad, gain_grad.reshape(C), shift_grad.reshape(C), bias_grad.reshape(C)
 
 

time: 48.1 us -> 46.9 us (0.975)
  Pallas kernels: 47.3 us -> 46.2 us
    pallas_call x1, Pallas kernels: 45.2 us -> 44.5 us  [body(): pl.pallas_call(kernel, out_shape=(pltpu.VMEM((NF, NR, W, C), BF16), pltpu...]
    pallas_call x1, Pallas kernels: 2.11 us -> 1.62 us  [body(): pl.pallas_call(write_out, out_shape=(jax.ShapeDtypeStruct((NF, NR, W, C),...]
where the time goes in v7:
time: 46.9 us; the launch traced here: 46.8 us
  Pallas kernels  46.2 us (99%)
  between operations  0.64 us (1%)
    pallas_call x1, Pallas kernels, body(): pl.pallas_call(kernel, out_shape=(pltpu.VMEM((NF, NR, W, C), BF16), pltpu...  44.5 us
    pallas_call x1, Pallas kernels, body(): pl.pallas_call(write_out, out_shape=(jax.ShapeDtypeStruct((NF, NR, W, C),...  1.62 us

profile of v7, /device:TPU:1, one launch (start us, length us, event | category | flops | bytes accessed | tf_op | source)
XLA Modules:
  0.0 46.8 jit_solution(18191042641130801155)
XLA Ops:
  0.6 44.5 %shard_map.92 = (bf16[4,8,128,128]{3,2,1,0:T(8,128)(2,1)S(1)}, f32[3,3,3,128,128]{4,3,2,1,0:T(8,128)S(1)}, f32[1,128]{1,0:T(1,128)S(1)}, f32[1,128]{1,0:T(1,128)S(1)}, f32[1,128]{1,0:T(1,128)S(1)}) custom-call(bf16[4,8,128,128]{3,2,1,0:T(8,128)(2,1)} %act_hbm.1, bf16[4,8,128,128]{3,2,1,0:T(8,128)(2,1)} %cot_hbm.1, bf16[9,384,128]{2,1,0:T(8,128)(2,1)} %bitcast.6, ...), custom_call_target="tpu_custom_call" | custom-call | tf_op jit(solution)/shard_map/pallas_call | solution.py:428
  45.2 1.6 %shard_map.93 = (bf16[4,8,128,128]{3,2,1,0:T(8,128)(2,1)}, f32[3,3,3,128,128]{4,3,2,1,0:T(8,128)}, f32[1,128]{1,0:T(1,128)}, f32[1,128]{1,0:T(1,128)}, f32[1,128]{1,0:T(1,128)}) custom-call(bf16[4,8,128,128]{3,2,1,0:T(8,128)(2,1)S(1)} %get-tuple-element.15.in_ref, f32[3,3,3,128,128]{4,3,2,1,0:T(8,128)S(1)} %get-tuple-element.16.w_ref, ...), custom_call_target="tpu_custom_call" | custom-call | tf_op jit(solution)/shard_map/pallas_call | solution.py:470

commit v8 on v7

--- a/solution.py
+++ b/solution.py
@@ -15,6 +15,7 @@
 SCALE = float(CELLS) ** -0.5
 SENT = 2 * NF * 64 + 2 * NR * 64 + 2 * (7 + 15) * 4 + 27 * 64 + 3 * 27 * 48 + 18 * 24 + 18 * 32 + 9 * 56
 GROUPS = 3
+FAR_FIRST = (2, 1, 3)
 NT_DIMS = (((1,), (1,)), ((), ()))
 
 
@@ -110,16 +111,17 @@
     def reduce_start(n, value):
         stat[n, 0] = value
         ara[n, xc] = value
-        for d in range(1, 8):
-            remote(stat.at[n, 0], ara.at[n, xc], send_sem.at[0], ar_r.at[n, 0], in_row((xc + d) % 8)).start()
+        for d in (4, 5, 2, 3, 6, 7, 1):
+            remote(stat.at[n, 0], ara.at[n, xc], send_sem.at[0], ar_r.at[n, 0], in_row((x + d // 2) % 4 * 2 + (core + d) % 2)).start()
 
     def reduce_middle(n):
         take(ara.at[n, pl.ds(0, 7)], ar_r.at[n, 0])
         value = ara[n].sum(axis=0)
         stat[n, 1] = value
         arb[n, yz] = value
-        for d in range(1, 16):
-            remote(stat.at[n, 1], arb.at[n, yz], send_sem.at[0], ar_r.at[n, 1], in_yz((yz + d) % 16)).start()
+        for d in (10, 6, 14, 9, 11, 5, 7, 13, 15, 8, 2, 4, 12, 1, 3):
+            to = (z + d // 4) % 4 * 4 + (y + d % 4) % 4
+            remote(stat.at[n, 1], arb.at[n, yz], send_sem.at[0], ar_r.at[n, 1], in_yz(to)).start()
 
     def reduce_end(n):
         take(arb.at[n, pl.ds(0, 15)], ar_r.at[n, 1])
@@ -136,7 +138,6 @@
         remote(grad_v.at[NF + 1, NR], grad_v.at[NF + 1, 0], send_sem.at[4], halo_r.at[5], below),
     ]
     before = ((span + 7) % 8, slab)
-    half = NR // 2
 
     def frame_send(f, start, size, n):
         to = grad_v.at[NF + f, pl.ds(1 + start, size)]
@@ -148,7 +149,7 @@
     reduce_start(0, stacked(one, two))
     halo[0].start()
     halo[1].start()
-    frame_send(0, 0, half, 0)
+    frame_send(0, 0, 5, 0)
 
     copy_cot.wait()
 
@@ -198,7 +199,7 @@
     act_grad(1, (2, 1, 0), False, inner)
     act_grad(2, (2, 1), False, inner)
     reduce_middle(0)
-    frame_send(0, half, half, 0)
+    frame_send(0, 5, NR - 5, 0)
     frame_send(1, 0, 1, 1)
     frame_send(1, NR - 1, 1, 1)
     frame_send(1, 1, NR - 2, 2)
@@ -263,7 +264,7 @@
         here = span_of(half0, 64)
         for b in range(3):
             wacc[b, at, here] = wacc[b, at, here] + rs_core[b, at]
-            for d in range(1, 4):
+            for d in FAR_FIRST:
                 k = (place[b] + d) % 4
                 src = wacc.at[b, at, span_of(half0 + k * 16, 16)]
                 to = rs_axis.at[0, b, place[b], at]
@@ -277,7 +278,7 @@
         axis = (b + k) % 3
         slot = rs_axis.at[k, b, place[axis], pl.ds(lo, hi - lo)]
         slot[...] = value
-        for d in range(1, 4):
+        for d in FAR_FIRST:
             remote(slot, slot, send_sem.at[0], recv.at[g, b], on_axis(axis, (place[axis] + d) % 4)).start()
 
     def along_second(g, b):
@@ -297,7 +298,7 @@
         total = rs_axis[2, b, :, lo:hi].sum(axis=0) * SCALE
         wout[b, lo:hi, mine(b)] = total.astype(BF16)
         tiles = wout.at[b, pl.ds(lo, hi - lo), mine(b)]
-        for d in range(1, 8) if g == 2 else (2, 4, 6):
+        for d in (4, 5, 2, 3, 6, 7, 1) if g == 2 else (4, 2, 6):
             to = on_axis(b, (place[b] + d // 2) % 4, (core + d) % 2)
             remote(tiles, tiles, send_sem.at[0], gx_r.at[g, b], to).start()
 

time: 46.9 us -> 46.6 us (level)
  no operation moved by 1% of the time
where the time goes in v8:
time: 46.6 us; the launch traced here: 46.5 us
  Pallas kernels  45.8 us (98%)
  between operations  0.64 us (1%)
    pallas_call x1, Pallas kernels, body(): pl.pallas_call(kernel, out_shape=(pltpu.VMEM((NF, NR, W, C), BF16), pltpu...  44.2 us
    pallas_call x1, Pallas kernels, body(): pl.pallas_call(write_out, out_shape=(jax.ShapeDtypeStruct((NF, NR, W, C),...  1.62 us

profile of v8, /device:TPU:1, one launch (start us, length us, event | category | flops | bytes accessed | tf_op | source)
XLA Modules:
  0.0 46.5 jit_solution(15406922774738291552)
XLA Ops:
  0.6 44.2 %shard_map.92 = (bf16[4,8,128,128]{3,2,1,0:T(8,128)(2,1)S(1)}, f32[3,3,3,128,128]{4,3,2,1,0:T(8,128)S(1)}, f32[1,128]{1,0:T(1,128)S(1)}, f32[1,128]{1,0:T(1,128)S(1)}, f32[1,128]{1,0:T(1,128)S(1)}) custom-call(bf16[4,8,128,128]{3,2,1,0:T(8,128)(2,1)} %act_hbm.1, bf16[4,8,128,128]{3,2,1,0:T(8,128)(2,1)} %cot_hbm.1, bf16[9,384,128]{2,1,0:T(8,128)(2,1)} %bitcast.6, ...), custom_call_target="tpu_custom_call" | custom-call | tf_op jit(solution)/shard_map/pallas_call | solution.py:429
  44.8 1.6 %shard_map.93 = (bf16[4,8,128,128]{3,2,1,0:T(8,128)(2,1)}, f32[3,3,3,128,128]{4,3,2,1,0:T(8,128)}, f32[1,128]{1,0:T(1,128)}, f32[1,128]{1,0:T(1,128)}, f32[1,128]{1,0:T(1,128)}) custom-call(bf16[4,8,128,128]{3,2,1,0:T(8,128)(2,1)S(1)} %get-tuple-element.15.in_ref, f32[3,3,3,128,128]{4,3,2,1,0:T(8,128)S(1)} %get-tuple-element.16.w_ref, ...), custom_call_target="tpu_custom_call" | custom-call | tf_op jit(solution)/shard_map/pallas_call | solution.py:471

commit v9 on v8

--- a/solution.py
+++ b/solution.py
@@ -147,9 +147,9 @@
         take(grad_v.at[NF, pl.ds(0, (NR, 2, NR - 2)[n])], frame_r.at[n])
 
     reduce_start(0, stacked(one, two))
+    frame_send(0, 0, 5, 0)
     halo[0].start()
     halo[1].start()
-    frame_send(0, 0, 5, 0)
 
     copy_cot.wait()
 

time: 46.6 us -> 46.5 us (level)
  no operation moved by 1% of the time
where the time goes in v9:
time: 46.5 us; the launch traced here: 46.4 us
  Pallas kernels  45.7 us (98%)
  between operations  0.64 us (1%)
    pallas_call x1, Pallas kernels, body(): pl.pallas_call(kernel, out_shape=(pltpu.VMEM((NF, NR, W, C), BF16), pltpu...  44.1 us
    pallas_call x1, Pallas kernels, body(): pl.pallas_call(write_out, out_shape=(jax.ShapeDtypeStruct((NF, NR, W, C),...  1.62 us

profile of v9, /device:TPU:1, one launch (start us, length us, event | category | flops | bytes accessed | tf_op | source)
XLA Modules:
  0.0 46.4 jit_solution(16891659450235114941)
XLA Ops:
  0.6 44.1 %shard_map.92 = (bf16[4,8,128,128]{3,2,1,0:T(8,128)(2,1)S(1)}, f32[3,3,3,128,128]{4,3,2,1,0:T(8,128)S(1)}, f32[1,128]{1,0:T(1,128)S(1)}, f32[1,128]{1,0:T(1,128)S(1)}, f32[1,128]{1,0:T(1,128)S(1)}) custom-call(bf16[4,8,128,128]{3,2,1,0:T(8,128)(2,1)} %act_hbm.1, bf16[4,8,128,128]{3,2,1,0:T(8,128)(2,1)} %cot_hbm.1, bf16[9,384,128]{2,1,0:T(8,128)(2,1)} %bitcast.6, ...), custom_call_target="tpu_custom_call" | custom-call | tf_op jit(solution)/shard_map/pallas_call | solution.py:429
  44.8 1.6 %shard_map.93 = (bf16[4,8,128,128]{3,2,1,0:T(8,128)(2,1)}, f32[3,3,3,128,128]{4,3,2,1,0:T(8,128)}, f32[1,128]{1,0:T(1,128)}, f32[1,128]{1,0:T(1,128)}, f32[1,128]{1,0:T(1,128)}) custom-call(bf16[4,8,128,128]{3,2,1,0:T(8,128)(2,1)S(1)} %get-tuple-element.15.in_ref, f32[3,3,3,128,128]{4,3,2,1,0:T(8,128)S(1)} %get-tuple-element.16.w_ref, ...), custom_call_target="tpu_custom_call" | custom-call | tf_op jit(solution)/shard_map/pallas_call | solution.py:471
